TPU v7x, 32 devices: a whole 2x2x4 slice. The times are simulated.
32 devices in a mesh: leaf: 8 (over z, core), front: 4 (over y, x).
Axes of the slice: x: 2, y: 2, z: 4, core: 2. Of those that a mesh axis runs over, the one named last changes fastest.
Arguments:
- blocks: bfloat16 [256, 128, 1024], P(('leaf', 'front')), may hold values from -0.1875 to 0.1875
- pattern: int32 [256, 8], P(('leaf', 'front')), may hold values 0 or 1
- assign: int32 [256, 1], P(('leaf', 'front')), may hold values from 0 to 7; in each aligned block of 8 rows (0 to 7, 8 to 15, ...) at most 2 rows name the same one
- order: int32 [8], replicated, may hold values from 0 to 7, each once
- leaf_map: int32 [8, 4], replicated, may hold values from 0 to 7, as said below
- mid_map: int32 [4, 4], replicated, may hold values from 0 to 7, as said below
- prior: float32 [8, 3, 1024], P('leaf'), may hold values from 1 to 4
Outputs:
- leaf_factor: float32 [8, 512, 1024], P('leaf', 'front')
- mid_factor: float32 [8, 256, 1024], P('leaf', 'front')
- top_factor: float32 [8, 256, 1024], P('leaf', 'front')
Inputs may be any that keep to these rules, and one draw needn't show every extreme that they name: `assign`: in each aligned block of 8 rows (the row blocks of one device) no front is named more than 2 times; in every draw some block names some front exactly 2 times, and every front is named somewhere. `leaf_map`: each row holds 4 distinct numbers; rows 2k and 2k+1 share exactly 2 numbers. `mid_map`: each row holds 4 distinct numbers; rows 2k and 2k+1 share exactly 2 numbers.
All inputs are finite; a program needn't handle non-finite values. No bound on the sum of `pattern` on one device may be relied on, other than what follows from the above.
Results may differ from a plain program's by a relative error of at most 0.0003.
Values may be sent and summed in bfloat16 or wider, within the bound.
A program may use at most 128 MiB of HBM per device.

v0:
```python
import functools
import jax
import jax.numpy as jnp
from jax import lax
from jax.experimental import pallas as pl
from jax.experimental.pallas import tpu as pltpu
from jax.sharding import PartitionSpec as P

CAP = 2
SUB = 8
HIGHEST = lax.Precision.HIGHEST


def partner(value, axis, stride):
    mask = 2**stride
    pairs = [(source, source ^ mask) for source in range(lax.axis_size(axis))]
    return lax.ppermute(value, axis, pairs)


def factor_tile(diagonal):
    size = diagonal.shape[0]
    tiles = size // SUB
    shape = (SUB, size)
    sub_ids = lax.broadcasted_iota(jnp.int32, shape, 0)
    lane_ids = lax.broadcasted_iota(jnp.int32, shape, 1)
    left = [diagonal[SUB * t : SUB * (t + 1), :] for t in range(tiles)]
    right = [(lane_ids == sub_ids + SUB * t).astype(jnp.float32) for t in range(tiles)]

    def lanes(tile, column):
        return jnp.broadcast_to(tile[:, column : column + 1], shape)

    def subs(tile, row):
        return jnp.broadcast_to(tile[row : row + 1, :], shape)

    for step in range(tiles):
        columns = [lanes(left[step], SUB * step + j) for j in range(SUB)]
        entry = [[subs(columns[j], i) for j in range(i + 1)] for i in range(SUB)]
        row_left = [subs(left[step], i) for i in range(SUB)]
        row_right = [subs(right[step], i) for i in range(SUB)]
        last = step == tiles - 1
        if not last:
            ahead = [lanes(left[step + 1], SUB * step + j) for j in range(SUB)]
            next_left, next_right = left[step + 1], right[step + 1]
        scale = []
        for p in range(SUB):
            inverse = lax.rsqrt(entry[p][p])
            scale.append(inverse)
            for i in range(p + 1, SUB):
                entry[i][p] = entry[i][p] * inverse
            row_left[p] = row_left[p] * inverse
            row_right[p] = row_right[p] * inverse
            for k in range(p + 1, SUB):
                for i in range(k, SUB):
                    entry[i][k] = entry[i][k] - entry[i][p] * entry[k][p]
                row_left[k] = row_left[k] - entry[k][p] * row_left[p]
                row_right[k] = row_right[k] - entry[k][p] * row_right[p]
            if not last:
                ahead[p] = ahead[p] * inverse
                next_left = next_left - ahead[p] * row_left[p]
                next_right = next_right - ahead[p] * row_right[p]
                for k in range(p + 1, SUB):
                    ahead[k] = ahead[k] - entry[k][p] * ahead[p]
        new_left, new_right = row_left[0], row_right[0]
        for p in range(1, SUB):
            new_left = jnp.where(sub_ids == p, row_left[p], new_left)
            new_right = jnp.where(sub_ids == p, row_right[p], new_right)
        left[step], right[step] = new_left, new_right
        if last:
            break
        left[step + 1], right[step + 1] = next_left, next_right
        for p in reversed(range(SUB)):
            for k in range(p + 1, SUB):
                row_left[p] = row_left[p] - entry[k][p] * row_left[k]
                row_right[p] = row_right[p] - entry[k][p] * row_right[k]
            row_left[p] = row_left[p] * scale[p]
            row_right[p] = row_right[p] * scale[p]
        for t in range(step + 2, tiles):
            new_left, new_right = left[t], right[t]
            for j in range(SUB):
                column = lanes(left[t], SUB * step + j)
                new_left = new_left - column * row_left[j]
                new_right = new_right - column * row_right[j]
            left[t], right[t] = new_left, new_right
    return jnp.concatenate(left, 0), jnp.concatenate(right, 0)


def halves(value):
    high = value.astype(jnp.bfloat16)
    return high, (value - high.astype(jnp.float32)).astype(jnp.bfloat16)


def product(left, right, contract):
    def dot(a, b):
        return lax.dot_general(
            a, b, (((contract,), (0,)), ((), ())), preferred_element_type=jnp.float32
        )

    return dot(left[0], right[0]) + (dot(left[0], right[1]) + dot(left[1], right[0]))


def eliminate(front, split, pivots, block):
    blocks = front.shape[0] // block

    def step(index, carry):
        start = pl.multiple_of(index * block, block)
        rows = pl.ds(start, block)
        upper, inverse = factor_tile(front[rows, rows])
        front[rows, :] = product(halves(inverse), halves(front[rows, :]), 1)
        front[rows, rows] = upper
        split[0], split[1] = halves(front[rows, :])

        def update(first, other, carry):
            below = pl.ds(pl.multiple_of(other * block, block), block)
            front[below, first:] = front[below, first:] - product(
                (split[0, :, below], split[1, :, below]), (split[0, :, first:], split[1, :, first:]), 0
            )
            return carry

        middle = blocks // 2
        lax.fori_loop(index + 1, middle, functools.partial(update, 0), carry)
        return lax.fori_loop(
            jnp.maximum(index + 1, middle), blocks,
            functools.partial(update, middle * block), carry,
        )

    lax.fori_loop(0, pivots // block, step, 0)


def add_weights(front, weights, block):
    size = front.shape[0]
    same = lax.broadcasted_iota(jnp.int32, (block, block), 0) == lax.broadcasted_iota(
        jnp.int32, (block, block), 1
    )
    for start in range(0, size, block):
        at = slice(start, start + block)
        front[at, at] = front[at, at] + jnp.where(same, weights[:, at], 0.0)


def take_rows(front, out, start):
    count, width = out.shape
    row_ids = start + lax.broadcasted_iota(jnp.int32, (count, width), 0)
    lane_ids = lax.broadcasted_iota(jnp.int32, (count, width), 1)
    out[...] = jnp.where(lane_ids >= row_ids, front[pl.ds(start, count), :], 0.0)


def pairs(count):
    return [(i, j) for i in range(count) for j in range(i, count)]


def pack_triangle(front, packed, first, block):
    count = front.shape[0] // block - first
    for index, (i, j) in enumerate(pairs(count)):
        rows, cols = (first + i) * block, (first + j) * block
        packed[index * block : (index + 1) * block, :] = front[
            rows : rows + block, cols : cols + block
        ]


def leaf_kernel(block, place, gram, weights, out, rest, front, split):
    width = front.shape[0]
    front[...] = jnp.zeros_like(front)
    for index, (i, j) in enumerate(pairs(width // block)):
        front[i * block : (i + 1) * block, j * block : (j + 1) * block] = gram[
            index * block : (index + 1) * block, :
        ]
    add_weights(front, weights, block)
    eliminate(front, split, width // 2, block)
    take_rows(front, out, pl.multiple_of(place[0] * out.shape[0], SUB))
    pack_triangle(front, rest, width // 2 // block, block)


def merge_kernel(block, pivots, place, maps, own, other, weights, out, *more):
    *more, front, split = more
    half = front.shape[0] // 2
    front[...] = jnp.zeros_like(front)
    add_weights(front, weights, block)
    for source, child in enumerate((own, other)):
        for index, (i, j) in enumerate(pairs(half // block)):
            tile = child[index * block : (index + 1) * block, :]
            first = pl.ds(pl.multiple_of(maps[source, i] * block, block), block)
            second = pl.ds(pl.multiple_of(maps[source, j] * block, block), block)
            front[first, second] = front[first, second] + tile
            if i != j:
                front[second, first] = front[second, first] + tile.T
    eliminate(front, split, pivots, block)
    take_rows(front, out, pl.multiple_of(place[0] * out.shape[0], SUB))
    if more:
        pack_triangle(front, more[0], half // block, block)


def gram_kernel(block, rows, packed):
    width = rows.shape[1]
    count = width // block
    where = {pair: index for index, pair in enumerate(pairs(count))}
    for i in range(0, count, 2):
        product = lax.dot_general(
            rows[:, i * block : (i + 2) * block], rows[:, i * block :],
            (((0,), (0,)), ((), ())), preferred_element_type=jnp.float32,
        )
        for k in (i, i + 1):
            for j in range(k, count):
                at = where[(k, j)] * block
                packed[at : at + block, :] = product[
                    (k - i) * block : (k - i + 1) * block, (j - i) * block : (j - i + 1) * block
                ]


def greet(devices):
    barrier = pltpu.get_barrier_semaphore()
    for device in devices:
        pl.semaphore_signal(
            barrier, inc=1, device_id=device, device_id_type=pl.DeviceIdType.MESH
        )
    pl.semaphore_wait(barrier, len(devices))


def remote(source, target, send, recv, device):
    copy = pltpu.make_async_remote_copy(
        src_ref=source, dst_ref=target, send_sem=send, recv_sem=recv,
        device_id=device, device_id_type=pl.DeviceIdType.MESH,
    )
    copy.start()
    return copy


def sum_kernel(fronts, part, out, total, full, landed, send, recv, send_back, recv_back):
    leaf, me = lax.axis_index("leaf"), lax.axis_index("front")
    strides = [2**level for level in range(fronts.bit_length() - 1)]
    sides = [lax.rem(me // stride, 2) for stride in strides]
    peers = [me + stride - 2 * stride * side for stride, side in zip(strides, sides)]
    levels = len(strides)
    half = part.shape[0] // 2
    orders = [list(range(levels)), list(reversed(range(levels)))]
    offset = [0, half]
    greet([(leaf, peer) for peer in peers])

    def at(start, size):
        return pl.ds(pl.multiple_of(start, SUB), size)

    size = half
    for level in range(levels):
        size = size // 2
        source = part if level == 0 else total
        copies, keeps = [], []
        for way in range(2):
            axis = orders[way][level]
            keeps.append(offset[way] + sides[axis] * size)
            slot = way * levels + level
            land = landed.at[pl.ds(way * half + half - 2 * size, size)]
            copies.append((
                remote(
                    source.at[at(offset[way] + (1 - sides[axis]) * size, size)], land,
                    send.at[slot], recv.at[slot], (leaf, peers[axis]),
                ),
                way * half + half - 2 * size,
            ))
        for way, (copy, place) in enumerate(copies):
            copy.wait()
            mine = at(keeps[way], size)
            result = full if level == levels - 1 else total
            result[mine, :] = source[mine, :] + landed[place : place + size, :]
            offset[way] = keeps[way]
    for level in reversed(range(levels)):
        copies = []
        for way in range(2):
            axis = orders[way][level]
            slot = way * levels + level
            mine = full.at[at(offset[way], size)]
            copies.append(
                remote(mine, mine, send_back.at[slot], recv_back.at[slot], (leaf, peers[axis]))
            )
            offset[way] = offset[way] - sides[axis] * size
        for copy in copies:
            copy.wait()
        size = size * 2
    out[...] = full[...]


def route_kernel(order, assign, pattern, blocks, out):
    leaves, positions = out.shape[:2]
    count, _, width = blocks.shape
    column_blocks = pattern.shape[1]
    block = width // column_blocks

    def slot_step(slot, carry):
        found = [jnp.int32(count)] * positions
        for b in range(count):
            free = assign[b] == order[slot]
            for p in range(positions):
                take = jnp.logical_and(free, found[p] == count)
                found[p] = jnp.where(take, b, found[p])
                free = jnp.logical_and(free, jnp.logical_not(take))
        for p in range(positions):
            source = jnp.minimum(found[p], count - 1)
            for c in range(column_blocks):
                keep = jnp.where(found[p] < count, pattern[source, c], 0)
                cols = slice(c * block, (c + 1) * block)
                scale = jnp.full((block, block), keep, jnp.int32).astype(jnp.float32)
                out[slot, p, :, cols] = blocks[source, :, cols] * scale.astype(out.dtype)
        return carry

    lax.fori_loop(0, leaves, slot_step, 0)


def swap_kernel(fronts, stride, own, out, got, send, recv, send_on, recv_on):
    leaf, me = lax.axis_index("leaf"), lax.axis_index("front")
    other = leaf + stride - 2 * stride * lax.rem(leaf // stride, 2)
    peers = [lax.rem(me + d, fronts) for d in range(1, fronts)]
    piece = own.shape[0] // fronts
    mine = pl.ds(pl.multiple_of(me * piece, SUB), piece)
    greet([(other, me)] + [(leaf, peer) for peer in peers])
    remote(own.at[mine], got.at[mine], send, recv, (other, me)).wait()
    copies = [
        remote(got.at[mine], got.at[mine], send_on.at[d], recv_on.at[d], (leaf, peer))
        for d, peer in enumerate(peers)
    ]
    for copy in copies:
        copy.wait()
    out[...] = got[...]


SMEM = pl.BlockSpec(memory_space=pltpu.SMEM)
VMEM = pl.BlockSpec(memory_space=pltpu.VMEM)


def route(order, assign, pattern, blocks, leaves):
    return pl.pallas_call(
        route_kernel,
        out_shape=jax.ShapeDtypeStruct((leaves, CAP) + blocks.shape[1:], blocks.dtype),
        in_specs=[SMEM, SMEM, SMEM, VMEM],
        out_specs=VMEM,
        compiler_params=pltpu.CompilerParams(vmem_limit_bytes=48 * 2**20),
        name="route_blocks",
    )(order, assign.reshape(-1), pattern, blocks)


def packed_gram(rows, block):
    count = rows.shape[1] // block
    return pl.pallas_call(
        functools.partial(gram_kernel, block),
        out_shape=jax.ShapeDtypeStruct((len(pairs(count)) * block, block), jnp.float32),
        in_specs=[VMEM],
        out_specs=VMEM,
        compiler_params=pltpu.CompilerParams(vmem_limit_bytes=48 * 2**20),
        name="packed_gram",
    )(rows)


def sum_fronts(part, fronts):
    size, width = part.shape
    many = pltpu.SemaphoreType.DMA((2 * (fronts.bit_length() - 1),))
    return pl.pallas_call(
        functools.partial(sum_kernel, fronts),
        out_shape=jax.ShapeDtypeStruct(part.shape, part.dtype),
        in_specs=[VMEM],
        out_specs=VMEM,
        scratch_shapes=[
            pltpu.VMEM((size, width), part.dtype),
            pltpu.VMEM((size, width), part.dtype),
            pltpu.VMEM((size, width), part.dtype),
            many, many, many, many,
        ],
        compiler_params=pltpu.CompilerParams(
            collective_id=0, has_side_effects=True, vmem_limit_bytes=48 * 2**20
        ),
        name="sum_fronts",
    )(part)


def swap_leaves(own, fronts, stride):
    many = pltpu.SemaphoreType.DMA((fronts - 1,))
    one = pltpu.SemaphoreType.DMA
    return pl.pallas_call(
        functools.partial(swap_kernel, fronts, stride),
        out_shape=jax.ShapeDtypeStruct(own.shape, own.dtype),
        in_specs=[VMEM],
        out_specs=VMEM,
        scratch_shapes=[pltpu.VMEM(own.shape, own.dtype), one, one, many, many],
        compiler_params=pltpu.CompilerParams(
            collective_id=1, has_side_effects=True, vmem_limit_bytes=48 * 2**20
        ),
        name="swap_leaves",
    )(own)


def triangle_shape(width, block):
    return jax.ShapeDtypeStruct((len(pairs(width // 2 // block)) * block, block), jnp.float32)


def leaf_level(gram, weights, place, rows, block):
    width = weights.shape[1]
    return pl.pallas_call(
        functools.partial(leaf_kernel, block),
        out_shape=(
            jax.ShapeDtypeStruct((rows, width), jnp.float32),
            triangle_shape(width, block),
        ),
        in_specs=[SMEM, VMEM, VMEM],
        out_specs=(VMEM, VMEM),
        scratch_shapes=[
            pltpu.VMEM((width, width), jnp.float32),
            pltpu.VMEM((2, block, width), jnp.bfloat16),
        ],
        compiler_params=pltpu.CompilerParams(vmem_limit_bytes=48 * 2**20),
        name="leaf_front",
    )(place.reshape(1).astype(jnp.int32), gram, weights)


def merge_level(own, other, maps, weights, place, rows, block, pivots, name):
    width = weights.shape[1]
    outs = [jax.ShapeDtypeStruct((rows, width), jnp.float32)]
    if pivots < width:
        outs.append(triangle_shape(width, block))
    return pl.pallas_call(
        functools.partial(merge_kernel, block, pivots),
        out_shape=tuple(outs),
        in_specs=[SMEM, SMEM, VMEM, VMEM, VMEM],
        out_specs=tuple([VMEM] * len(outs)),
        scratch_shapes=[
            pltpu.VMEM((width, width), jnp.float32),
            pltpu.VMEM((2, block, width), jnp.bfloat16),
        ],
        compiler_params=pltpu.CompilerParams(vmem_limit_bytes=48 * 2**20),
        name=name,
    )(place.reshape(1).astype(jnp.int32), maps, own, other, weights)


def local(blocks, pattern, assign, order, leaf_map, mid_map, prior):
    leaves = lax.axis_size("leaf")
    fronts = lax.axis_size("front")
    slot_index = lax.axis_index("leaf")
    front_index = lax.axis_index("front")
    local_blocks, block_size, full_width = blocks.shape
    half_width = full_width // 2
    quarter = full_width // 4
    carried = prior[0, 1:3]
    carried = carried + partner(carried, "leaf", 0)
    top_weights = carried[1:2] + partner(carried[1:2], "leaf", 1)
    outgoing = route(order, assign, pattern, blocks, leaves)
    arrived = lax.all_to_all(outgoing, "leaf", split_axis=0, concat_axis=0, tiled=True)
    arrived_rows = arrived.reshape(-1, full_width)
    gram = sum_fronts(packed_gram(arrived_rows, block_size), fronts)
    leaf_out, rest = leaf_level(
        gram, prior[0, 0:1], front_index, half_width // fronts, block_size
    )
    piece_rows = quarter // fronts
    partner_slot = jnp.bitwise_xor(slot_index, 1)
    mid_out, mid_rest = merge_level(
        rest,
        partner(rest, "leaf", 0),
        jnp.stack([leaf_map[slot_index], leaf_map[partner_slot]]),
        carried[0:1],
        slot_index % 2 * fronts + front_index,
        piece_rows,
        block_size,
        half_width,
        "mid_front",
    )
    middle = slot_index // 2
    other_middle = jnp.bitwise_xor(slot_index, 2) // 2
    (top_out,) = merge_level(
        mid_rest,
        swap_leaves(mid_rest, fronts, 2),
        jnp.stack([mid_map[middle], mid_map[other_middle]]),
        top_weights,
        slot_index % 4 * fronts + front_index,
        piece_rows,
        block_size,
        full_width,
        "top_front",
    )
    return (leaf_out[None], mid_out[None], top_out[None])


def solution(mesh):
    placed = (
        P(("leaf", "front"), None, None),
        P(("leaf", "front"), None),
        P(("leaf", "front"), None),
        P(),
        P(),
        P(),
        P("leaf", None, None),
    )
    return jax.shard_map(
        local,
        mesh=mesh,
        in_specs=placed,
        out_specs=(P("leaf", "front", None), P("leaf", "front", None), P("leaf", "front", None)),
        check_vma=False,
    )
```

profile of v0, /device:TPU:0, one launch (start us, length us, event | category | flops | bytes accessed | tf_op | source)
XLA Modules:
  0.0 283.9 jit_solution(2354105966414562841)
XLA Ops:
  0.6 0.0 copy-start
  0.6 1.6 copy-done
  2.2 0.0 copy-start.1
  2.2 0.7 copy-done.1
  2.9 0.0 copy-start.2
  2.9 0.7 copy-done.2
  3.6 0.0 copy-start.3
  3.6 0.7 copy-done.3
  4.2 3.8 %route_blocks.1 = bf16[8,2,128,1024]{3,2,1,0:T(8,128)(2,1)} custom-call(s32[8]{0:T(128)S(1)} %copy-done.2, s32[8]{0:T(128)S(1)} %bitcast.15, s32[8,8]{1,0:T(8,128)S(1)} %copy-done.1, bf16[8,128,1024]{2,1,0:T(8,128)(2,1)S(1)} %copy-done), custom_call_target="tpu_custom_call" | custom-call | tf_op jit(solution)/shard_map/route_blocks/pallas_call | solution.py:327
  8.0 0.0 copy-start.4
  8.0 0.0 copy-start.5
  8.0 6.5 %all-to-all-start = ((bf16[8,2,128,1024]{3,2,1,0:T(8,128)(2,1)}), bf16[8,2,128,1024]{3,2,1,0:T(8,128)(2,1)}, u32[]{:S(2)}, u32[]{:S(2)}) async-start(bf16[8,2,128,1024]{3,2,1,0:T(8,128)(2,1)} %route_blocks.1), calls=%async_computation | async-start | bytes 8388608 | tf_op jit(solution)/shard_map/all_to_all | solution.py:440
  14.5 0.0 copy-done.4
  14.5 0.6 collective-permute-start.1
  15.1 0.0 copy-done.5
  15.1 0.1 constant_dynamic-slice_fusion.3
  15.1 0.1 copy.14
  15.2 0.1 copy.13
  15.4 93.2 %all-to-all-done = bf16[8,2,128,1024]{3,2,1,0:T(8,128)(2,1)} async-done(((bf16[8,2,128,1024]{3,2,1,0:T(8,128)(2,1)}), bf16[8,2,128,1024]{3,2,1,0:T(8,128)(2,1)}, u32[]{:S(2)}, u32[]{:S(2)}) %all-to-all-start) | async-done | bytes 4194336 | tf_op jit(solution)/shard_map/all_to_all | solution.py:440
  108.6 5.1 %packed_gram.1.part = f32[4608,128]{1,0:T(8,128)S(1)} custom-call(bf16[2048,1024]{1,0:T(8,128)(2,1)} %bitcast.2.rows), custom_call_target="tpu_custom_call" | custom-call | tf_op jit(solution)/shard_map/packed_gram/pallas_call | solution.py:339
  113.7 42.1 %sum_fronts.1.gram = f32[4608,128]{1,0:T(8,128)S(1)} custom-call(f32[4608,128]{1,0:T(8,128)S(1)} %packed_gram.1.part), custom_call_target="tpu_custom_call" | custom-call | tf_op jit(solution)/shard_map/sum_fronts/pallas_call | solution.py:352
  155.7 0.0 copy-start.6
  155.7 29.1 %leaf_front.1 = (f32[128,1024]{1,0:T(8,128)}, f32[1280,128]{1,0:T(8,128)S(1)}) custom-call(s32[1]{0:T(128)} %bitcast.place, f32[4608,128]{1,0:T(8,128)S(1)} %sum_fronts.1.gram, f32[1,1024]{1,0:T(1,128)S(1)} %slice_bitcast_fusion.weights), custom_call_target="tpu_custom_call" | custom-call | tf_op jit(solution)/shard_map/leaf_front/pallas_call | solution.py:392
  184.8 0.0 collective-permute-start
  184.8 0.0 copy-done.6
  184.8 0.0 collective-permute-done.1
  184.9 0.1 collective-permute-start.2
  185.0 3.5 %collective-permute-done.2 = f32[1,1024]{1,0:T(1,128)S(1)} collective-permute-done((f32[1,1024]{1,0:T(1,128)S(1)}, f32[1,1024]{1,0:T(1,128)S(1)}, u32[]{:S(2)}, u32[]{:S(2)}) %collective-permute-start.2) | collective-permute-done | bytes 4128 | tf_op jit(solution)/shard_map/ppermute | solution.py:17
  188.6 0.0 collective-permute-done.other
  188.6 30.1 %mid_front.1 = (f32[64,1024]{1,0:T(8,128)}, f32[1280,128]{1,0:T(8,128)S(1)}) custom-call(s32[1]{0:T(128)} %bitcast.5.place, s32[2,4]{1,0:T(2,128)S(1)} %pad_add_fusion.maps, f32[1280,128]{1,0:T(8,128)S(1)} %get-tuple-element.8.own, f32[1280,128]{1,0:T(8,128)S(1)} %collective-permute-done.other, f32[1,1024]{1,0:T(1,128)S(1)} %get-tuple-element.12.weights), custom_call_target="tpu_custom_call" | custom-call | tf_op jit(solution)/shard_map/mid_front/pallas_call | solution.py:414
  218.7 13.0 %swap_leaves.1.other = f32[1280,128]{1,0:T(8,128)S(1)} custom-call(f32[1280,128]{1,0:T(8,128)S(1)} %get-tuple-element.10.own), custom_call_target="tpu_custom_call" | custom-call | tf_op jit(solution)/shard_map/swap_leaves/pallas_call | solution.py:373
  231.6 52.3 %top_front.1 = f32[64,1024]{1,0:T(8,128)} custom-call(s32[1]{0:T(128)} %bitcast.8.place, s32[2,4]{1,0:T(2,128)S(1)} %pad_add_fusion.1.maps, f32[1280,128]{1,0:T(8,128)S(1)} %get-tuple-element.10.own, f32[1280,128]{1,0:T(8,128)S(1)} %swap_leaves.1.other, f32[1,1024]{1,0:T(1,128)S(1)} %get-tuple-element.11.weights), custom_call_target="tpu_custom_call" | custom-call | tf_op jit(solution)/shard_map/top_front/pallas_call | solution.py:414
  (9 shorter events, 0.1 us)
Async XLA Ops:
  0.6 1.6 copy-start
  2.2 0.7 copy-start.1
  2.9 0.7 copy-start.2
  3.6 0.7 copy-start.3
  8.0 6.5 %copy-start.4 = (f32[1,3,1024]{2,0,1:T(1,128)S(1)}, f32[1,3,1024]{2,0,1:T(1,128)}, u32[]{:S(2)}) copy-start(f32[1,3,1024]{2,0,1:T(1,128)} %param.13) | copy-start | bytes 36868
  8.0 7.1 %copy-start.5 = (s32[8,4]{0,1:T(4,128)S(1)}, s32[8,4]{0,1:T(4,128)}, u32[]{:S(2)}) copy-start(s32[8,4]{0,1:T(4,128)} %param.11) | copy-start | bytes 388
  8.0 100.6 %all-to-all-start = ((bf16[8,2,128,1024]{3,2,1,0:T(8,128)(2,1)}), bf16[8,2,128,1024]{3,2,1,0:T(8,128)(2,1)}, u32[]{:S(2)}, u32[]{:S(2)}) async-start(bf16[8,2,128,1024]{3,2,1,0:T(8,128)(2,1)} %route_blocks.1), calls=%async_computation | async-start | bytes 8388608 | tf_op jit(solution)/shard_map/all_to_all | solution.py:440
  14.5 170.3 %collective-permute-start.1 = (f32[2,1024]{1,0:T(2,128)S(1)}, f32[2,1024]{1,0:T(2,128)S(1)}, u32[]{:S(2)}, u32[]{:S(2)}) collective-permute-start(f32[2,1024]{1,0:T(2,128)S(1)} %bitcast.17), channel_id=1, source_target_pairs={{0,4},{4,0},{8,12},{12,8},{16,20},{20,16},{24,28},{28,24},{1,5},{5... | collective-permute-start | bytes 24584 | tf_op jit(solution)/shard_map/ppermute | solution.py:17
  155.7 29.1 %copy-start.6 = (s32[4,4]{1,0:T(4,128)S(1)}, s32[4,4]{1,0:T(4,128)}, u32[]{:S(2)}) copy-start(s32[4,4]{1,0:T(4,128)} %param.12) | copy-start | bytes 196
  184.8 3.7 %collective-permute-start = (f32[1280,128]{1,0:T(8,128)S(1)}, f32[1280,128]{1,0:T(8,128)S(1)}, u32[]{:S(2)}, u32[]{:S(2)}) collective-permute-start(f32[1280,128]{1,0:T(8,128)S(1)} %get-tuple-element.8.own), channel_id=1, source_target_pairs={{0,4},{4,0},{8,12},{12,8},{16,20},{20,16},{24,28},{28,24},{1,5},{5... | collective-permute-start | bytes 1966088 | tf_op jit(solution)/shard_map/ppermute | solution.py:17
  184.9 3.7 %collective-permute-start.2 = (f32[1,1024]{1,0:T(1,128)S(1)}, f32[1,1024]{1,0:T(1,128)S(1)}, u32[]{:S(2)}, u32[]{:S(2)}) collective-permute-start(f32[1,1024]{1,0:T(1,128)S(1)} %slice.18), channel_id=1, source_target_pairs={{0,8},{4,12},{8,0},{12,4},{16,24},{20,28},{24,16},{28,20},{1,9},{5... | collective-permute-start | bytes 12296 | tf_op jit(solution)/shard_map/ppermute | solution.py:17
where the time goes:
time: 284 us
  Pallas kernels  175 us (62%)
  waiting for transfers between devices  96.8 us (34%)
  starting transfers between devices  7.17 us (3%)
  local copies, waits for them, and re-layouts  3.88 us (1%)
    all_to_all x1, waiting for transfers between devices, local(): lax.all_to_all(outgoing, 'leaf', split_axis=0, concat_axis=0, tiled=True)  93.2 us
    pallas_call x2, Pallas kernels, merge_level(): pl.pallas_call(functools.partial(merge_kernel, block, pivots), out_shape=...  82.4 us
    pallas_call x1, Pallas kernels, sum_fronts(): pl.pallas_call(functools.partial(sum_kernel, fronts), out_shape=jax.Shape...  42.1 us
    pallas_call x1, Pallas kernels, leaf_level(): pl.pallas_call(functools.partial(leaf_kernel, block), out_shape=(jax.Shap...  29.1 us
    pallas_call x1, Pallas kernels, swap_leaves(): pl.pallas_call(functools.partial(swap_kernel, fronts, stride), out_shape=...  13 us
    all_to_all x1, starting transfers between devices, local(): lax.all_to_all(outgoing, 'leaf', split_axis=0, concat_axis=0, tiled=True)  6.49 us
  transfers between devices with their start and end apart: 4, of which 2 were waited for; matrix products, arithmetic and copies ran while one was open for 0% of the time, Pallas kernels for 27%

commit v1 on v0

--- a/solution.py
+++ b/solution.py
@@ -8,6 +8,7 @@
 
 CAP = 2
 SUB = 8
+NEAR = 3
 HIGHEST = lax.Precision.HIGHEST
 
 
@@ -15,6 +16,14 @@
     mask = 2**stride
     pairs = [(source, source ^ mask) for source in range(lax.axis_size(axis))]
     return lax.ppermute(value, axis, pairs)
+
+
+def lanes(tile, column):
+    return jnp.broadcast_to(tile[:, column : column + 1], tile.shape)
+
+
+def subs(tile, row):
+    return jnp.broadcast_to(tile[row : row + 1, :], tile.shape)
 
 
 def factor_tile(diagonal):
@@ -23,65 +32,62 @@
     shape = (SUB, size)
     sub_ids = lax.broadcasted_iota(jnp.int32, shape, 0)
     lane_ids = lax.broadcasted_iota(jnp.int32, shape, 1)
+    picks = [sub_ids == p for p in range(SUB)]
     left = [diagonal[SUB * t : SUB * (t + 1), :] for t in range(tiles)]
     right = [(lane_ids == sub_ids + SUB * t).astype(jnp.float32) for t in range(tiles)]
-
-    def lanes(tile, column):
-        return jnp.broadcast_to(tile[:, column : column + 1], shape)
-
-    def subs(tile, row):
-        return jnp.broadcast_to(tile[row : row + 1, :], shape)
-
+    zero = left[0] * 0.0
+    upper, inverse = [], []
+
+    def columns_of(t, step):
+        return [lanes(left[t], SUB * step + j) for j in range(SUB)]
+
+    own = [column + zero for column in columns_of(0, 0)]
     for step in range(tiles):
-        columns = [lanes(left[step], SUB * step + j) for j in range(SUB)]
-        entry = [[subs(columns[j], i) for j in range(i + 1)] for i in range(SUB)]
-        row_left = [subs(left[step], i) for i in range(SUB)]
-        row_right = [subs(right[step], i) for i in range(SUB)]
-        last = step == tiles - 1
-        if not last:
-            ahead = [lanes(left[step + 1], SUB * step + j) for j in range(SUB)]
-            next_left, next_right = left[step + 1], right[step + 1]
-        scale = []
+        own_left, own_right = left[step], right[step]
+        row_left, row_right = own_left, own_right
+        near = range(step + 1, min(step + 1 + NEAR, tiles))
+        ahead = {t: columns_of(t, step) for t in near}
+        following = None
+        if step + 1 < tiles:
+            following = [column + zero for column in columns_of(step + 1, step + 1)]
         for p in range(SUB):
-            inverse = lax.rsqrt(entry[p][p])
-            scale.append(inverse)
-            for i in range(p + 1, SUB):
-                entry[i][p] = entry[i][p] * inverse
-            row_left[p] = row_left[p] * inverse
-            row_right[p] = row_right[p] * inverse
+            scale = lax.rsqrt(subs(own[p], p))
+            squared = scale * scale
+            ratio = [None] * SUB
             for k in range(p + 1, SUB):
-                for i in range(k, SUB):
-                    entry[i][k] = entry[i][k] - entry[i][p] * entry[k][p]
-                row_left[k] = row_left[k] - entry[k][p] * row_left[p]
-                row_right[k] = row_right[k] - entry[k][p] * row_right[p]
-            if not last:
-                ahead[p] = ahead[p] * inverse
-                next_left = next_left - ahead[p] * row_left[p]
-                next_right = next_right - ahead[p] * row_right[p]
+                row = subs(own[k], p)
+                ratio[k] = row * squared
+                if k == p + 1:
+                    own[k] = own[k] - (own[p] * row) * squared
+                else:
+                    own[k] = own[k] - own[p] * ratio[k]
+            pivot_left, pivot_right = subs(own_left, p), subs(own_right, p)
+            row_left = jnp.where(picks[p], pivot_left * scale, row_left)
+            row_right = jnp.where(picks[p], pivot_right * scale, row_right)
+            pivot_left, pivot_right = pivot_left * squared, pivot_right * squared
+            if p < SUB - 1:
+                own_left = own_left - own[p] * pivot_left
+                own_right = own_right - own[p] * pivot_right
+            if following is not None:
+                scaled = ahead[step + 1][p] * squared
+                for k in range(SUB):
+                    following[k] = following[k] - ahead[step + 1][p] * subs(scaled, k)
+            for t in near:
+                left[t] = left[t] - ahead[t][p] * pivot_left
+                right[t] = right[t] - ahead[t][p] * pivot_right
                 for k in range(p + 1, SUB):
-                    ahead[k] = ahead[k] - entry[k][p] * ahead[p]
-        new_left, new_right = row_left[0], row_right[0]
-        for p in range(1, SUB):
-            new_left = jnp.where(sub_ids == p, row_left[p], new_left)
-            new_right = jnp.where(sub_ids == p, row_right[p], new_right)
-        left[step], right[step] = new_left, new_right
-        if last:
-            break
-        left[step + 1], right[step + 1] = next_left, next_right
-        for p in reversed(range(SUB)):
-            for k in range(p + 1, SUB):
-                row_left[p] = row_left[p] - entry[k][p] * row_left[k]
-                row_right[p] = row_right[p] - entry[k][p] * row_right[k]
-            row_left[p] = row_left[p] * scale[p]
-            row_right[p] = row_right[p] * scale[p]
-        for t in range(step + 2, tiles):
-            new_left, new_right = left[t], right[t]
-            for j in range(SUB):
-                column = lanes(left[t], SUB * step + j)
-                new_left = new_left - column * row_left[j]
-                new_right = new_right - column * row_right[j]
-            left[t], right[t] = new_left, new_right
-    return jnp.concatenate(left, 0), jnp.concatenate(right, 0)
+                    ahead[t][k] = ahead[t][k] - ahead[t][p] * ratio[k]
+        upper.append(row_left)
+        inverse.append(row_right)
+        own = following
+        if step + 1 + NEAR < tiles:
+            high, low = halves(jnp.concatenate([row_left, row_right], 1))
+            change = product((high[:, :size], low[:, :size]), (high, low), 0)
+            for t in range(step + 1 + NEAR, tiles):
+                rows = slice(SUB * t, SUB * (t + 1))
+                left[t] = left[t] - change[rows, :size]
+                right[t] = right[t] - change[rows, size:]
+    return jnp.concatenate(upper, 0), jnp.concatenate(inverse, 0)
 
 
 def halves(value):
@@ -90,38 +96,62 @@
 
 
 def product(left, right, contract):
-    def dot(a, b):
-        return lax.dot_general(
-            a, b, (((contract,), (0,)), ((), ())), preferred_element_type=jnp.float32
-        )
-
-    return dot(left[0], right[0]) + (dot(left[0], right[1]) + dot(left[1], right[0]))
-
-
-def eliminate(front, split, pivots, block):
+    return lax.dot_general(
+        jnp.concatenate([left[0], left[0], left[1]], contract),
+        jnp.concatenate([right[0], right[1], right[0]], 0),
+        (((contract,), (0,)), ((), ())),
+        preferred_element_type=jnp.float32,
+    )
+
+
+def eliminate(front, split, pivots, block, touched=None):
     blocks = front.shape[0] // block
 
     def step(index, carry):
         start = pl.multiple_of(index * block, block)
         rows = pl.ds(start, block)
-        upper, inverse = factor_tile(front[rows, rows])
-        front[rows, :] = product(halves(inverse), halves(front[rows, :]), 1)
-        front[rows, rows] = upper
-        split[0], split[1] = halves(front[rows, :])
-
-        def update(first, other, carry):
-            below = pl.ds(pl.multiple_of(other * block, block), block)
-            front[below, first:] = front[below, first:] - product(
-                (split[0, :, below], split[1, :, below]), (split[0, :, first:], split[1, :, first:]), 0
+
+        def dense():
+            upper, inverse = factor_tile(front[rows, rows])
+            front[rows, :] = product(halves(inverse), halves(front[rows, :]), 1)
+            front[rows, rows] = upper
+            split[0], split[1] = halves(front[rows, :])
+
+            def update(first, other, carry):
+                below = pl.ds(pl.multiple_of(other * block, block), block)
+
+                def apply():
+                    front[below, first:] = front[below, first:] - product(
+                        (split[0, :, below], split[1, :, below]), (split[0, :, first:], split[1, :, first:]), 0
+                    )
+
+                if touched is None:
+                    apply()
+                else:
+                    pl.when(touched(other))(apply)
+                return carry
+
+            middle = blocks // 2
+            lax.fori_loop(index + 1, middle, functools.partial(update, 0), 0)
+            lax.fori_loop(
+                jnp.maximum(index + 1, middle), blocks,
+                functools.partial(update, middle * block), 0,
             )
-            return carry
-
-        middle = blocks // 2
-        lax.fori_loop(index + 1, middle, functools.partial(update, 0), carry)
-        return lax.fori_loop(
-            jnp.maximum(index + 1, middle), blocks,
-            functools.partial(update, middle * block), carry,
-        )
+
+        if touched is None:
+            dense()
+        else:
+            here = touched(index)
+            pl.when(here)(dense)
+
+            @pl.when(jnp.logical_not(here))
+            def _():
+                tile = front[rows, rows]
+                shape = (block, block)
+                same = lax.broadcasted_iota(jnp.int32, shape, 0) == lax.broadcasted_iota(jnp.int32, shape, 1)
+                front[rows, rows] = jnp.where(same, tile * lax.rsqrt(tile), 0.0)
+
+        return carry
 
     lax.fori_loop(0, pivots // block, step, 0)
 
@@ -182,7 +212,15 @@
             front[first, second] = front[first, second] + tile
             if i != j:
                 front[second, first] = front[second, first] + tile.T
-    eliminate(front, split, pivots, block)
+
+    def touched(index):
+        found = maps[0, 0] == index
+        for source in range(2):
+            for i in range(half // block):
+                found = jnp.logical_or(found, maps[source, i] == index)
+        return found
+
+    eliminate(front, split, pivots, block, touched)
     take_rows(front, out, pl.multiple_of(place[0] * out.shape[0], SUB))
     if more:
         pack_triangle(front, more[0], half // block, block)

time: 284 us -> 234 us (0.82); the launches traced: 284 us -> 230 us
  Pallas kernels: 175 us -> 122 us
    pallas_call x2, Pallas kernels: 82.4 us -> 38.8 us  [merge_level(): pl.pallas_call(functools.partial(merge_kernel, block, pivots), out_shape=...]
    pallas_call x1, Pallas kernels: 29.1 us -> 19.1 us  [leaf_level(): pl.pallas_call(functools.partial(leaf_kernel, block), out_shape=(jax.Shap...]
  transfers between devices with their start and end apart: 4 -> 4, of which waited for: 2 -> 2; matrix products, arithmetic and copies ran while one was open for 0% -> 0% of each run, Pallas kernels for 27% -> 29%
where the time goes in v1:
time: 234 us; the launch traced here: 230 us
  Pallas kernels  122 us (52%)
  waiting for transfers between devices  96.7 us (41%)
  starting transfers between devices  7.19 us (3%)
  local copies, waits for them, and re-layouts  3.88 us (2%)
    all_to_all x1, waiting for transfers between devices, local(): lax.all_to_all(outgoing, 'leaf', split_axis=0, concat_axis=0, tiled=True)  93.2 us
    pallas_call x1, Pallas kernels, sum_fronts(): pl.pallas_call(functools.partial(sum_kernel, fronts), out_shape=jax.Shape...  42.1 us
    pallas_call x2, Pallas kernels, merge_level(): pl.pallas_call(functools.partial(merge_kernel, block, pivots), out_shape=...  38.8 us
    pallas_call x1, Pallas kernels, leaf_level(): pl.pallas_call(functools.partial(leaf_kernel, block), out_shape=(jax.Shap...  19.1 us
    pallas_call x1, Pallas kernels, swap_leaves(): pl.pallas_call(functools.partial(swap_kernel, fronts, stride), out_shape=...  13 us
    all_to_all x1, starting transfers between devices, local(): lax.all_to_all(outgoing, 'leaf', split_axis=0, concat_axis=0, tiled=True)  6.49 us
    pallas_call x1, Pallas kernels, packed_gram(): pl.pallas_call(functools.partial(gram_kernel, block), out_shape=jax.Shape...  5.08 us
  transfers between devices with their start and end apart: 4, of which 2 were waited for; matrix products, arithmetic and copies ran while one was open for 0% of the time, Pallas kernels for 29%

profile of v1, /device:TPU:0, one launch (start us, length us, event | category | flops | bytes accessed | tf_op | source)
XLA Modules:
  0.0 230.4 jit_solution(15914546783515805040)
XLA Ops:
  0.6 0.0 copy-start
  0.6 1.6 copy-done
  2.2 0.0 copy-start.1
  2.2 0.7 copy-done.1
  2.9 0.0 copy-start.2
  2.9 0.7 copy-done.2
  3.6 0.0 copy-start.3
  3.6 0.7 copy-done.3
  4.2 3.8 %route_blocks.1 = bf16[8,2,128,1024]{3,2,1,0:T(8,128)(2,1)} custom-call(s32[8]{0:T(128)S(1)} %copy-done.2, s32[8]{0:T(128)S(1)} %bitcast.15, s32[8,8]{1,0:T(8,128)S(1)} %copy-done.1, bf16[8,128,1024]{2,1,0:T(8,128)(2,1)S(1)} %copy-done), custom_call_target="tpu_custom_call" | custom-call | tf_op jit(solution)/shard_map/route_blocks/pallas_call | solution.py:365
  8.0 0.0 copy-start.4
  8.0 0.0 copy-start.5
  8.0 6.5 %all-to-all-start = ((bf16[8,2,128,1024]{3,2,1,0:T(8,128)(2,1)}), bf16[8,2,128,1024]{3,2,1,0:T(8,128)(2,1)}, u32[]{:S(2)}, u32[]{:S(2)}) async-start(bf16[8,2,128,1024]{3,2,1,0:T(8,128)(2,1)} %route_blocks.1), calls=%async_computation | async-start | bytes 8388608 | tf_op jit(solution)/shard_map/all_to_all | solution.py:478
  14.5 0.0 copy-done.4
  14.5 0.6 collective-permute-start.1
  15.1 0.0 copy-done.5
  15.1 0.1 constant_dynamic-slice_fusion.3
  15.1 0.1 copy.14
  15.2 0.1 copy.13
  15.4 93.2 %all-to-all-done = bf16[8,2,128,1024]{3,2,1,0:T(8,128)(2,1)} async-done(((bf16[8,2,128,1024]{3,2,1,0:T(8,128)(2,1)}), bf16[8,2,128,1024]{3,2,1,0:T(8,128)(2,1)}, u32[]{:S(2)}, u32[]{:S(2)}) %all-to-all-start) | async-done | bytes 4194336 | tf_op jit(solution)/shard_map/all_to_all | solution.py:478
  108.6 5.1 %packed_gram.1.part = f32[4608,128]{1,0:T(8,128)S(1)} custom-call(bf16[2048,1024]{1,0:T(8,128)(2,1)} %bitcast.2.rows), custom_call_target="tpu_custom_call" | custom-call | tf_op jit(solution)/shard_map/packed_gram/pallas_call | solution.py:377
  113.7 42.1 %sum_fronts.1.gram = f32[4608,128]{1,0:T(8,128)S(1)} custom-call(f32[4608,128]{1,0:T(8,128)S(1)} %packed_gram.1.part), custom_call_target="tpu_custom_call" | custom-call | tf_op jit(solution)/shard_map/sum_fronts/pallas_call | solution.py:390
  155.7 0.0 copy-start.6
  155.7 19.1 %leaf_front.1 = (f32[128,1024]{1,0:T(8,128)}, f32[1280,128]{1,0:T(8,128)S(1)}) custom-call(s32[1]{0:T(128)} %bitcast.place, f32[4608,128]{1,0:T(8,128)S(1)} %sum_fronts.1.gram, f32[1,1024]{1,0:T(1,128)S(1)} %slice_bitcast_fusion.weights), custom_call_target="tpu_custom_call" | custom-call | tf_op jit(solution)/shard_map/leaf_front/pallas_call | solution.py:430
  174.8 0.0 collective-permute-start
  174.8 0.0 copy-done.6
  174.8 0.0 collective-permute-done.1
  174.9 0.1 collective-permute-start.2
  175.0 3.5 %collective-permute-done.2 = f32[1,1024]{1,0:T(1,128)S(1)} collective-permute-done((f32[1,1024]{1,0:T(1,128)S(1)}, f32[1,1024]{1,0:T(1,128)S(1)}, u32[]{:S(2)}, u32[]{:S(2)}) %collective-permute-start.2) | collective-permute-done | bytes 4128 | tf_op jit(solution)/shard_map/ppermute | solution.py:18
  178.6 0.0 collective-permute-done.other
  178.6 14.4 %mid_front.1 = (f32[64,1024]{1,0:T(8,128)}, f32[1280,128]{1,0:T(8,128)S(1)}) custom-call(s32[1]{0:T(128)} %bitcast.5.place, s32[2,4]{1,0:T(2,128)S(1)} %pad_add_fusion.maps, f32[1280,128]{1,0:T(8,128)S(1)} %get-tuple-element.8.own, f32[1280,128]{1,0:T(8,128)S(1)} %collective-permute-done.other, f32[1,1024]{1,0:T(1,128)S(1)} %get-tuple-element.12.weights), custom_call_target="tpu_custom_call" | custom-call | tf_op jit(solution)/shard_map/mid_front/pallas_call | solution.py:452
  193.0 13.0 %swap_leaves.1.other = f32[1280,128]{1,0:T(8,128)S(1)} custom-call(f32[1280,128]{1,0:T(8,128)S(1)} %get-tuple-element.10.own), custom_call_target="tpu_custom_call" | custom-call | tf_op jit(solution)/shard_map/swap_leaves/pallas_call | solution.py:411
  206.0 24.4 %top_front.1 = f32[64,1024]{1,0:T(8,128)} custom-call(s32[1]{0:T(128)} %bitcast.8.place, s32[2,4]{1,0:T(2,128)S(1)} %pad_add_fusion.1.maps, f32[1280,128]{1,0:T(8,128)S(1)} %get-tuple-element.10.own, f32[1280,128]{1,0:T(8,128)S(1)} %swap_leaves.1.other, f32[1,1024]{1,0:T(1,128)S(1)} %get-tuple-element.11.weights), custom_call_target="tpu_custom_call" | custom-call | tf_op jit(solution)/shard_map/top_front/pallas_call | solution.py:452
  (9 shorter events, 0.1 us)
Async XLA Ops:
  0.6 1.6 copy-start
  2.2 0.7 copy-start.1
  2.9 0.7 copy-start.2
  3.6 0.7 copy-start.3
  8.0 6.5 %copy-start.4 = (f32[1,3,1024]{2,0,1:T(1,128)S(1)}, f32[1,3,1024]{2,0,1:T(1,128)}, u32[]{:S(2)}) copy-start(f32[1,3,1024]{2,0,1:T(1,128)} %param.13) | copy-start | bytes 36868
  8.0 7.1 %copy-start.5 = (s32[8,4]{0,1:T(4,128)S(1)}, s32[8,4]{0,1:T(4,128)}, u32[]{:S(2)}) copy-start(s32[8,4]{0,1:T(4,128)} %param.11) | copy-start | bytes 388
  8.0 100.6 %all-to-all-start = ((bf16[8,2,128,1024]{3,2,1,0:T(8,128)(2,1)}), bf16[8,2,128,1024]{3,2,1,0:T(8,128)(2,1)}, u32[]{:S(2)}, u32[]{:S(2)}) async-start(bf16[8,2,128,1024]{3,2,1,0:T(8,128)(2,1)} %route_blocks.1), calls=%async_computation | async-start | bytes 8388608 | tf_op jit(solution)/shard_map/all_to_all | solution.py:478
  14.5 160.3 %collective-permute-start.1 = (f32[2,1024]{1,0:T(2,128)S(1)}, f32[2,1024]{1,0:T(2,128)S(1)}, u32[]{:S(2)}, u32[]{:S(2)}) collective-permute-start(f32[2,1024]{1,0:T(2,128)S(1)} %bitcast.17), channel_id=1, source_target_pairs={{0,4},{4,0},{8,12},{12,8},{16,20},{20,16},{24,28},{28,24},{1,5},{5... | collective-permute-start | bytes 24584 | tf_op jit(solution)/shard_map/ppermute | solution.py:18
  155.7 19.1 %copy-start.6 = (s32[4,4]{1,0:T(4,128)S(1)}, s32[4,4]{1,0:T(4,128)}, u32[]{:S(2)}) copy-start(s32[4,4]{1,0:T(4,128)} %param.12) | copy-start | bytes 196
  174.8 3.7 %collective-permute-start = (f32[1280,128]{1,0:T(8,128)S(1)}, f32[1280,128]{1,0:T(8,128)S(1)}, u32[]{:S(2)}, u32[]{:S(2)}) collective-permute-start(f32[1280,128]{1,0:T(8,128)S(1)} %get-tuple-element.8.own), channel_id=1, source_target_pairs={{0,4},{4,0},{8,12},{12,8},{16,20},{20,16},{24,28},{28,24},{1,5},{5... | collective-permute-start | bytes 1966088 | tf_op jit(solution)/shard_map/ppermute | solution.py:18
  174.9 3.7 %collective-permute-start.2 = (f32[1,1024]{1,0:T(1,128)S(1)}, f32[1,1024]{1,0:T(1,128)S(1)}, u32[]{:S(2)}, u32[]{:S(2)}) collective-permute-start(f32[1,1024]{1,0:T(1,128)S(1)} %slice.18), channel_id=1, source_target_pairs={{0,8},{4,12},{8,0},{12,4},{16,24},{20,28},{24,16},{28,20},{1,9},{5... | collective-permute-start | bytes 12296 | tf_op jit(solution)/shard_map/ppermute | solution.py:18

commit v2 on v1

--- a/solution.py
+++ b/solution.py
@@ -226,7 +226,7 @@
         pack_triangle(front, more[0], half // block, block)
 
 
-def gram_kernel(block, rows, packed):
+def gram_tiles(block, rows, packed):
     width = rows.shape[1]
     count = width // block
     where = {pair: index for index, pair in enumerate(pairs(count))}
@@ -261,43 +261,85 @@
     return copy
 
 
-def sum_kernel(fronts, part, out, total, full, landed, send, recv, send_back, recv_back):
+def sum_kernel(
+    leaves, fronts, block, rows, out, far_rows, own_rows, far, own, landed, swapped, full,
+    far_send, far_recv, own_send, own_recv, kept, send, recv, swap_send, swap_recv, send_back, recv_back,
+):
     leaf, me = lax.axis_index("leaf"), lax.axis_index("front")
+    team = leaves // 2
+    side, mate = leaf // team, lax.rem(leaf, team)
+    here, there = side * team, (1 - side) * team
+    depth = far_rows.shape[0] // team
     strides = [2**level for level in range(fronts.bit_length() - 1)]
     sides = [lax.rem(me // stride, 2) for stride in strides]
-    peers = [me + stride - 2 * stride * side for stride, side in zip(strides, sides)]
+    peers = [me + stride - 2 * stride * turn for stride, turn in zip(strides, sides)]
     levels = len(strides)
-    half = part.shape[0] // 2
+    half = far.shape[0] // 2
     orders = [list(range(levels)), list(reversed(range(levels)))]
-    offset = [0, half]
-    greet([(leaf, peer) for peer in peers])
+    mates = [lax.rem(mate + d, team) for d in range(1, team)]
+    opposite = there + mate
+    greet([(here + other, me) for other in mates] + [(opposite, me)] + [(leaf, peer) for peer in peers])
 
     def at(start, size):
         return pl.ds(pl.multiple_of(start, SUB), size)
 
-    size = half
-    for level in range(levels):
-        size = size // 2
-        source = part if level == 0 else total
-        copies, keeps = [], []
-        for way in range(2):
-            axis = orders[way][level]
-            keeps.append(offset[way] + sides[axis] * size)
-            slot = way * levels + level
-            land = landed.at[pl.ds(way * half + half - 2 * size, size)]
-            copies.append((
-                remote(
-                    source.at[at(offset[way] + (1 - sides[axis]) * size, size)], land,
-                    send.at[slot], recv.at[slot], (leaf, peers[axis]),
-                ),
-                way * half + half - 2 * size,
-            ))
-        for way, (copy, place) in enumerate(copies):
-            copy.wait()
-            mine = at(keeps[way], size)
-            result = full if level == levels - 1 else total
-            result[mine, :] = source[mine, :] + landed[place : place + size, :]
-            offset[way] = keeps[way]
+    def gather(base, target, send, recv, slot):
+        place = target.at[at(mate * depth, depth)]
+        copies = [
+            remote(rows.at[at((base + other) * depth, depth)], place, send.at[d], recv.at[d], (here + other, me))
+            for d, other in enumerate(mates)
+        ]
+        stay = pltpu.make_async_copy(rows.at[at((base + mate) * depth, depth)], place, kept.at[slot])
+        stay.start()
+        return copies + [stay]
+
+    def scatter(part, which):
+        offset = [0, half]
+        size = half
+        for level in range(levels):
+            size = size // 2
+            copies = []
+            for way in range(2):
+                axis = orders[way][level]
+                keep = offset[way] + sides[axis] * size
+                slot = (which * 2 + way) * levels + level
+                place = way * half + half - 2 * size
+                copies.append((
+                    remote(
+                        part.at[at(offset[way] + (1 - sides[axis]) * size, size)],
+                        landed.at[which, pl.ds(place, size)],
+                        send.at[slot], recv.at[slot], (leaf, peers[axis]),
+                    ),
+                    place,
+                ))
+                offset[way] = keep
+            for way, (copy, place) in enumerate(copies):
+                copy.wait()
+                mine = at(offset[way], size)
+                part[mine, :] = part[mine, :] + landed[which, place : place + size, :]
+        return offset, size
+
+    far_copies = gather(there, far_rows, far_send, far_recv, 0)
+    own_copies = gather(here, own_rows, own_send, own_recv, 1)
+    for copy in far_copies:
+        copy.wait()
+    gram_tiles(block, far_rows, far)
+    offset, size = scatter(far, 0)
+    swaps = [
+        remote(
+            far.at[at(offset[way], size)], swapped.at[pl.ds(way * size, size)],
+            swap_send.at[way], swap_recv.at[way], (opposite, me),
+        )
+        for way in range(2)
+    ]
+    for copy in own_copies:
+        copy.wait()
+    gram_tiles(block, own_rows, own)
+    offset, size = scatter(own, 1)
+    for way, copy in enumerate(swaps):
+        copy.wait()
+        mine = at(offset[way], size)
+        full[mine, :] = own[mine, :] + swapped[way * size : (way + 1) * size, :]
     for level in reversed(range(levels)):
         copies = []
         for way in range(2):
@@ -372,37 +414,38 @@
     )(order, assign.reshape(-1), pattern, blocks)
 
 
-def packed_gram(rows, block):
-    count = rows.shape[1] // block
+def gathered_gram(rows, leaves, fronts, block):
+    width = rows.shape[1]
+    packed = (len(pairs(width // block)) * block, block)
+    team = leaves // 2
+    levels = fronts.bit_length() - 1
+    half_rows = (rows.shape[0] // 2, width)
+
+    def many(count):
+        return pltpu.SemaphoreType.DMA((count,))
+
     return pl.pallas_call(
-        functools.partial(gram_kernel, block),
-        out_shape=jax.ShapeDtypeStruct((len(pairs(count)) * block, block), jnp.float32),
-        in_specs=[VMEM],
-        out_specs=VMEM,
-        compiler_params=pltpu.CompilerParams(vmem_limit_bytes=48 * 2**20),
-        name="packed_gram",
-    )(rows)
-
-
-def sum_fronts(part, fronts):
-    size, width = part.shape
-    many = pltpu.SemaphoreType.DMA((2 * (fronts.bit_length() - 1),))
-    return pl.pallas_call(
-        functools.partial(sum_kernel, fronts),
-        out_shape=jax.ShapeDtypeStruct(part.shape, part.dtype),
+        functools.partial(sum_kernel, leaves, fronts, block),
+        out_shape=jax.ShapeDtypeStruct(packed, jnp.float32),
         in_specs=[VMEM],
         out_specs=VMEM,
         scratch_shapes=[
-            pltpu.VMEM((size, width), part.dtype),
-            pltpu.VMEM((size, width), part.dtype),
-            pltpu.VMEM((size, width), part.dtype),
-            many, many, many, many,
+            pltpu.VMEM(half_rows, rows.dtype),
+            pltpu.VMEM(half_rows, rows.dtype),
+            pltpu.VMEM(packed, jnp.float32),
+            pltpu.VMEM(packed, jnp.float32),
+            pltpu.VMEM((2,) + packed, jnp.float32),
+            pltpu.VMEM((packed[0] // fronts, block), jnp.float32),
+            pltpu.VMEM(packed, jnp.float32),
+            many(team - 1), many(team - 1), many(team - 1), many(team - 1), many(2),
+            many(4 * levels), many(4 * levels), many(2), many(2),
+            many(2 * levels), many(2 * levels),
         ],
         compiler_params=pltpu.CompilerParams(
-            collective_id=0, has_side_effects=True, vmem_limit_bytes=48 * 2**20
+            collective_id=0, has_side_effects=True, vmem_limit_bytes=56 * 2**20
         ),
-        name="sum_fronts",
-    )(part)
+        name="gathered_gram",
+    )(rows)
 
 
 def swap_leaves(own, fronts, stride):
@@ -475,9 +518,7 @@
     carried = carried + partner(carried, "leaf", 0)
     top_weights = carried[1:2] + partner(carried[1:2], "leaf", 1)
     outgoing = route(order, assign, pattern, blocks, leaves)
-    arrived = lax.all_to_all(outgoing, "leaf", split_axis=0, concat_axis=0, tiled=True)
-    arrived_rows = arrived.reshape(-1, full_width)
-    gram = sum_fronts(packed_gram(arrived_rows, block_size), fronts)
+    gram = gathered_gram(outgoing.reshape(-1, full_width), leaves, fronts, block_size)
     leaf_out, rest = leaf_level(
         gram, prior[0, 0:1], front_index, half_width // fronts, block_size
     )

time: 234 us -> 193 us (0.82); the launches traced: 230 us -> 192 us
  waiting for transfers between devices: 96.7 us -> 4.83 us
  Pallas kernels: 122 us -> 180 us
  starting transfers between devices: 7.19 us -> 0.58 us
    all_to_all x1 -> x0, waiting for transfers between devices: 93.2 us -> none  [local(): lax.all_to_all(outgoing, 'leaf', split_axis=0, concat_axis=0, tiled=True)]
    pallas_call x2 -> x1, Pallas kernels: 47.1 us -> 107 us  [gathered_gram(): pl.pallas_call(functools.partial(sum_kernel, leaves, fronts, block), out_...]
    all_to_all x1 -> x0, starting transfers between devices: 6.49 us -> none  [local(): lax.all_to_all(outgoing, 'leaf', split_axis=0, concat_axis=0, tiled=True)]
    unnamed x17 -> x19, local copies, waits for them, and re-layouts: 3.79 us -> 5.45 us
  transfers between devices with their start and end apart: 4 -> 3, of which waited for: 2 -> 2; matrix products, arithmetic and copies ran while one was open for 0% -> 0% of each run, Pallas kernels for 29% -> 0%
where the time goes in v2:
time: 193 us; the launch traced here: 192 us
  Pallas kernels  180 us (93%)
  local copies, waits for them, and re-layouts  5.54 us (3%)
  waiting for transfers between devices  4.83 us (3%)
    pallas_call x1, Pallas kernels, gathered_gram(): pl.pallas_call(functools.partial(sum_kernel, leaves, fronts, block), out_...  107 us
    pallas_call x2, Pallas kernels, merge_level(): pl.pallas_call(functools.partial(merge_kernel, block, pivots), out_shape=...  38.5 us
    pallas_call x1, Pallas kernels, leaf_level(): pl.pallas_call(functools.partial(leaf_kernel, block), out_shape=(jax.Shap...  19.1 us
    pallas_call x1, Pallas kernels, swap_leaves(): pl.pallas_call(functools.partial(swap_kernel, fronts, stride), out_shape=...  11.8 us
    unnamed x19, local copies, waits for them, and re-layouts  5.45 us
    ppermute x3, waiting for transfers between devices, partner(): return lax.ppermute(value, axis, pairs)  4.83 us
  transfers between devices with their start and end apart: 3, of which 2 were waited for; matrix products, arithmetic and copies ran while one was open for 0% of the time, Pallas kernels for 0%

profile of v2, /device:TPU:0, one launch (start us, length us, event | category | flops | bytes accessed | tf_op | source)
XLA Modules:
  0.0 192.2 jit_solution(4437578938185733767)
XLA Ops:
  0.6 0.0 copy-start.1
  0.6 1.6 copy-done.1
  2.2 0.0 copy-start.2
  2.2 0.7 copy-done.2
  2.9 0.0 copy-start.3
  2.9 0.7 copy-done.3
  3.6 0.0 copy-start.4
  3.6 0.7 copy-done.4
  4.2 3.8 %route_blocks.1 = bf16[8,2,128,1024]{3,2,1,0:T(8,128)(2,1)} custom-call(s32[8]{0:T(128)S(1)} %copy-done.3, s32[8]{0:T(128)S(1)} %bitcast.15, s32[8,8]{1,0:T(8,128)S(1)} %copy-done.2, bf16[8,128,1024]{2,1,0:T(8,128)(2,1)S(1)} %copy-done.1), custom_call_target="tpu_custom_call" | custom-call | tf_op jit(solution)/shard_map/route_blocks/pallas_call | solution.py:407
  8.0 0.0 copy-start.5
  8.0 107.2 %gathered_gram.1.gram = f32[4608,128]{1,0:T(8,128)} custom-call(bf16[2048,1024]{1,0:T(8,128)(2,1)} %bitcast.16), custom_call_target="tpu_custom_call" | custom-call | tf_op jit(solution)/shard_map/gathered_gram/pallas_call | solution.py:427
  115.2 0.0 copy-done.5
  115.2 0.0 copy-start.6
  115.3 0.0 copy-start.7
  115.3 0.0 copy-start
  115.3 1.7 copy-done
  116.9 19.1 %leaf_front.1 = (f32[128,1024]{1,0:T(8,128)}, f32[1280,128]{1,0:T(8,128)S(1)}) custom-call(s32[1]{0:T(128)} %bitcast.place, f32[4608,128]{1,0:T(8,128)S(1)} %copy-done, f32[1,1024]{1,0:T(1,128)S(1)} %slice_bitcast_fusion.weights), custom_call_target="tpu_custom_call" | custom-call | tf_op jit(solution)/shard_map/leaf_front/pallas_call | solution.py:473
  136.1 0.0 collective-permute-start
  136.1 0.5 collective-permute-start.1
  136.6 0.0 copy-done.6
  136.6 0.1 constant_dynamic-slice_fusion.3
  136.7 0.1 copy.14
  136.7 0.1 copy.13
  136.9 0.0 copy-done.7
  136.9 1.3 collective-permute-done.1
  138.2 0.1 collective-permute-start.2
  138.3 3.6 %collective-permute-done.2 = f32[1,1024]{1,0:T(1,128)S(1)} collective-permute-done((f32[1,1024]{1,0:T(1,128)S(1)}, f32[1,1024]{1,0:T(1,128)S(1)}, u32[]{:S(2)}, u32[]{:S(2)}) %collective-permute-start.2) | collective-permute-done | bytes 4128 | tf_op jit(solution)/shard_map/ppermute | solution.py:18
  141.9 0.0 collective-permute-done.other
  141.9 14.4 %mid_front.1 = (f32[64,1024]{1,0:T(8,128)}, f32[1280,128]{1,0:T(8,128)S(1)}) custom-call(s32[1]{0:T(128)} %bitcast.5.place, s32[2,4]{1,0:T(2,128)S(1)} %pad_add_fusion.maps, f32[1280,128]{1,0:T(8,128)S(1)} %get-tuple-element.8.own, f32[1280,128]{1,0:T(8,128)S(1)} %collective-permute-done.other, f32[1,1024]{1,0:T(1,128)S(1)} %get-tuple-element.12.weights), custom_call_target="tpu_custom_call" | custom-call | tf_op jit(solution)/shard_map/mid_front/pallas_call | solution.py:495
  156.3 11.8 %swap_leaves.1.other = f32[1280,128]{1,0:T(8,128)S(1)} custom-call(f32[1280,128]{1,0:T(8,128)S(1)} %get-tuple-element.10.own), custom_call_target="tpu_custom_call" | custom-call | tf_op jit(solution)/shard_map/swap_leaves/pallas_call | solution.py:454
  168.1 24.1 %top_front.1 = f32[64,1024]{1,0:T(8,128)} custom-call(s32[1]{0:T(128)} %bitcast.8.place, s32[2,4]{1,0:T(2,128)S(1)} %pad_add_fusion.1.maps, f32[1280,128]{1,0:T(8,128)S(1)} %get-tuple-element.10.own, f32[1280,128]{1,0:T(8,128)S(1)} %swap_leaves.1.other, f32[1,1024]{1,0:T(1,128)S(1)} %get-tuple-element.11.weights), custom_call_target="tpu_custom_call" | custom-call | tf_op jit(solution)/shard_map/top_front/pallas_call | solution.py:495
  (9 shorter events, 0.1 us)
Async XLA Ops:
  0.6 1.6 copy-start.1
  2.2 0.7 copy-start.2
  2.9 0.7 copy-start.3
  3.6 0.7 copy-start.4
  8.0 107.2 %copy-start.5 = (f32[1,3,1024]{2,0,1:T(1,128)S(1)}, f32[1,3,1024]{2,0,1:T(1,128)}, u32[]{:S(2)}) copy-start(f32[1,3,1024]{2,0,1:T(1,128)} %param.13) | copy-start | bytes 36868
  115.2 21.3 %copy-start.6 = (s32[8,4]{0,1:T(4,128)S(1)}, s32[8,4]{0,1:T(4,128)}, u32[]{:S(2)}) copy-start(s32[8,4]{0,1:T(4,128)} %param.11) | copy-start | bytes 388
  115.3 21.6 %copy-start.7 = (s32[4,4]{1,0:T(4,128)S(1)}, s32[4,4]{1,0:T(4,128)}, u32[]{:S(2)}) copy-start(s32[4,4]{1,0:T(4,128)} %param.12) | copy-start | bytes 196
  115.3 1.7 copy-start
  136.1 5.8 %collective-permute-start = (f32[1280,128]{1,0:T(8,128)S(1)}, f32[1280,128]{1,0:T(8,128)S(1)}, u32[]{:S(2)}, u32[]{:S(2)}) collective-permute-start(f32[1280,128]{1,0:T(8,128)S(1)} %get-tuple-element.8.own), channel_id=1, source_target_pairs={{0,4},{4,0},{8,12},{12,8},{16,20},{20,16},{24,28},{28,24},{1,5},{5... | collective-permute-start | bytes 1966088 | tf_op jit(solution)/shard_map/ppermute | solution.py:18
  136.1 2.1 %collective-permute-start.1 = (f32[2,1024]{1,0:T(2,128)S(1)}, f32[2,1024]{1,0:T(2,128)S(1)}, u32[]{:S(2)}, u32[]{:S(2)}) collective-permute-start(f32[2,1024]{1,0:T(2,128)S(1)} %bitcast.18), channel_id=1, source_target_pairs={{0,4},{4,0},{8,12},{12,8},{16,20},{20,16},{24,28},{28,24},{1,5},{5... | collective-permute-start | bytes 24584 | tf_op jit(solution)/shard_map/ppermute | solution.py:18
  138.2 3.7 %collective-permute-start.2 = (f32[1,1024]{1,0:T(1,128)S(1)}, f32[1,1024]{1,0:T(1,128)S(1)}, u32[]{:S(2)}, u32[]{:S(2)}) collective-permute-start(f32[1,1024]{1,0:T(1,128)S(1)} %slice.18), channel_id=1, source_target_pairs={{0,8},{4,12},{8,0},{12,4},{16,24},{20,28},{24,16},{28,20},{1,9},{5... | collective-permute-start | bytes 12296 | tf_op jit(solution)/shard_map/ppermute | solution.py:18

commit v3 on v2

--- a/solution.py
+++ b/solution.py
@@ -95,48 +95,54 @@
     return high, (value - high.astype(jnp.float32)).astype(jnp.bfloat16)
 
 
-def product(left, right, contract):
-    return lax.dot_general(
+def stacked(left, right, contract):
+    return (
         jnp.concatenate([left[0], left[0], left[1]], contract),
         jnp.concatenate([right[0], right[1], right[0]], 0),
-        (((contract,), (0,)), ((), ())),
-        preferred_element_type=jnp.float32,
-    )
-
-
-def eliminate(front, split, pivots, block, touched=None):
-    blocks = front.shape[0] // block
-
-    def step(index, carry):
+    )
+
+
+def dot(left, right, contract):
+    return lax.dot_general(
+        left, right, (((contract,), (0,)), ((), ())), preferred_element_type=jnp.float32
+    )
+
+
+def product(left, right, contract):
+    return dot(*stacked(left, right, contract), contract)
+
+
+def eliminate(front, diagonal, over, under, pivots, block, touched=None):
+    width = front.shape[0]
+    blocks = width // block
+    shape = (block, block)
+    same = lax.broadcasted_iota(jnp.int32, shape, 0) == lax.broadcasted_iota(jnp.int32, shape, 1)
+    lane_ids = lax.broadcasted_iota(jnp.int32, (block, width), 1)
+
+    def put_off(first):
+        start = first
+        while start < blocks:
+            stop = min(start + 2, blocks)
+            rows = slice(start * block, stop * block)
+            front[rows, start * block :] = front[rows, start * block :] - dot(
+                over[:, rows], under[:, start * block :], 0
+            )
+            start = stop
+
+    def step(first, index, carry):
         start = pl.multiple_of(index * block, block)
         rows = pl.ds(start, block)
+        after = pl.ds(pl.multiple_of(jnp.minimum(index + 1, blocks - 1) * block, block), block)
 
         def dense():
-            upper, inverse = factor_tile(front[rows, rows])
-            front[rows, :] = product(halves(inverse), halves(front[rows, :]), 1)
+            upper, inverse = factor_tile(diagonal[...])
+            put_off(first)
+            row = product(halves(inverse), halves(front[rows, :]), 1)
+            front[rows, :] = row
             front[rows, rows] = upper
-            split[0], split[1] = halves(front[rows, :])
-
-            def update(first, other, carry):
-                below = pl.ds(pl.multiple_of(other * block, block), block)
-
-                def apply():
-                    front[below, first:] = front[below, first:] - product(
-                        (split[0, :, below], split[1, :, below]), (split[0, :, first:], split[1, :, first:]), 0
-                    )
-
-                if touched is None:
-                    apply()
-                else:
-                    pl.when(touched(other))(apply)
-                return carry
-
-            middle = blocks // 2
-            lax.fori_loop(index + 1, middle, functools.partial(update, 0), 0)
-            lax.fori_loop(
-                jnp.maximum(index + 1, middle), blocks,
-                functools.partial(update, middle * block), 0,
-            )
+            parts = halves(jnp.where(lane_ids >= start + block, row, 0.0))
+            over[...], under[...] = stacked(parts, parts, 0)
+            diagonal[...] = front[after, after] - dot(over[:, after], under[:, after], 0)
 
         if touched is None:
             dense()
@@ -146,14 +152,33 @@
 
             @pl.when(jnp.logical_not(here))
             def _():
+                put_off(first)
                 tile = front[rows, rows]
-                shape = (block, block)
-                same = lax.broadcasted_iota(jnp.int32, shape, 0) == lax.broadcasted_iota(jnp.int32, shape, 1)
                 front[rows, rows] = jnp.where(same, tile * lax.rsqrt(tile), 0.0)
+                over[...] = jnp.zeros_like(over)
+                under[...] = jnp.zeros_like(under)
+                diagonal[...] = front[after, after]
 
         return carry
 
-    lax.fori_loop(0, pivots // block, step, 0)
+    over[...] = jnp.zeros_like(over)
+    under[...] = jnp.zeros_like(under)
+    diagonal[...] = front[:block, :block]
+    panels = pivots // block
+    middle = min(panels, blocks // 2)
+    lax.fori_loop(0, middle, functools.partial(step, 1), 0)
+    if middle < panels:
+        lax.fori_loop(middle, panels, functools.partial(step, middle), 0)
+    put_off(panels)
+
+
+def work(width, block):
+    return [
+        pltpu.VMEM((width, width), jnp.float32),
+        pltpu.VMEM((block, block), jnp.float32),
+        pltpu.VMEM((3 * block, width), jnp.bfloat16),
+        pltpu.VMEM((3 * block, width), jnp.bfloat16),
+    ]
 
 
 def add_weights(front, weights, block):
@@ -186,7 +211,7 @@
         ]
 
 
-def leaf_kernel(block, place, gram, weights, out, rest, front, split):
+def leaf_kernel(block, place, gram, weights, out, rest, front, diagonal, over, under):
     width = front.shape[0]
     front[...] = jnp.zeros_like(front)
     for index, (i, j) in enumerate(pairs(width // block)):
@@ -194,13 +219,13 @@
             index * block : (index + 1) * block, :
         ]
     add_weights(front, weights, block)
-    eliminate(front, split, width // 2, block)
+    eliminate(front, diagonal, over, under, width // 2, block)
     take_rows(front, out, pl.multiple_of(place[0] * out.shape[0], SUB))
     pack_triangle(front, rest, width // 2 // block, block)
 
 
 def merge_kernel(block, pivots, place, maps, own, other, weights, out, *more):
-    *more, front, split = more
+    *more, front, diagonal, over, under = more
     half = front.shape[0] // 2
     front[...] = jnp.zeros_like(front)
     add_weights(front, weights, block)
@@ -220,7 +245,7 @@
                 found = jnp.logical_or(found, maps[source, i] == index)
         return found
 
-    eliminate(front, split, pivots, block, touched)
+    eliminate(front, diagonal, over, under, pivots, block, touched)
     take_rows(front, out, pl.multiple_of(place[0] * out.shape[0], SUB))
     if more:
         pack_triangle(front, more[0], half // block, block)
@@ -478,10 +503,7 @@
         ),
         in_specs=[SMEM, VMEM, VMEM],
         out_specs=(VMEM, VMEM),
-        scratch_shapes=[
-            pltpu.VMEM((width, width), jnp.float32),
-            pltpu.VMEM((2, block, width), jnp.bfloat16),
-        ],
+        scratch_shapes=work(width, block),
         compiler_params=pltpu.CompilerParams(vmem_limit_bytes=48 * 2**20),
         name="leaf_front",
     )(place.reshape(1).astype(jnp.int32), gram, weights)
@@ -497,10 +519,7 @@
         out_shape=tuple(outs),
         in_specs=[SMEM, SMEM, VMEM, VMEM, VMEM],
         out_specs=tuple([VMEM] * len(outs)),
-        scratch_shapes=[
-            pltpu.VMEM((width, width), jnp.float32),
-            pltpu.VMEM((2, block, width), jnp.bfloat16),
-        ],
+        scratch_shapes=work(width, block),
         compiler_params=pltpu.CompilerParams(vmem_limit_bytes=48 * 2**20),
         name=name,
     )(place.reshape(1).astype(jnp.int32), maps, own, other, weights)

time: 193 us -> 187 us (0.969)
  Pallas kernels: 180 us -> 175 us
    pallas_call x2, Pallas kernels: 38.5 us -> 34.3 us  [merge_level(): pl.pallas_call(functools.partial(merge_kernel, block, pivots), out_shape=...]
    pallas_call x1, Pallas kernels: 19.1 us -> 15 us  [leaf_level(): pl.pallas_call(functools.partial(leaf_kernel, block), out_shape=(jax.Shap...]
    pallas_call x1, Pallas kernels: 11.8 us -> 14.3 us  [swap_leaves(): pl.pallas_call(functools.partial(swap_kernel, fronts, stride), out_shape=...]
where the time goes in v3:
time: 187 us; the launch traced here: 186 us
  Pallas kernels  175 us (94%)
  local copies, waits for them, and re-layouts  5.54 us (3%)
  waiting for transfers between devices  4.83 us (3%)
    pallas_call x1, Pallas kernels, gathered_gram(): pl.pallas_call(functools.partial(sum_kernel, leaves, fronts, block), out_...  107 us
    pallas_call x2, Pallas kernels, merge_level(): pl.pallas_call(functools.partial(merge_kernel, block, pivots), out_shape=...  34.3 us
    pallas_call x1, Pallas kernels, leaf_level(): pl.pallas_call(functools.partial(leaf_kernel, block), out_shape=(jax.Shap...  15 us
    pallas_call x1, Pallas kernels, swap_leaves(): pl.pallas_call(functools.partial(swap_kernel, fronts, stride), out_shape=...  14.3 us
    unnamed x19, local copies, waits for them, and re-layouts  5.45 us
    ppermute x3, waiting for transfers between devices, partner(): return lax.ppermute(value, axis, pairs)  4.83 us
    pallas_call x1, Pallas kernels, route(): pl.pallas_call(route_kernel, out_shape=jax.ShapeDtypeStruct((leaves, CAP)...  3.75 us
  transfers between devices with their start and end apart: 3, of which 2 were waited for; matrix products, arithmetic and copies ran while one was open for 0% of the time, Pallas kernels for 0%

profile of v3, /device:TPU:0, one launch (start us, length us, event | category | flops | bytes accessed | tf_op | source)
XLA Modules:
  0.0 186.3 jit_solution(1152609102498460497)
XLA Ops:
  0.6 0.0 copy-start.1
  0.6 1.6 copy-done.1
  2.2 0.0 copy-start.2
  2.2 0.7 copy-done.2
  2.9 0.0 copy-start.3
  2.9 0.7 copy-done.3
  3.6 0.0 copy-start.4
  3.6 0.7 copy-done.4
  4.2 3.8 %route_blocks.1 = bf16[8,2,128,1024]{3,2,1,0:T(8,128)(2,1)} custom-call(s32[8]{0:T(128)S(1)} %copy-done.3, s32[8]{0:T(128)S(1)} %bitcast.15, s32[8,8]{1,0:T(8,128)S(1)} %copy-done.2, bf16[8,128,1024]{2,1,0:T(8,128)(2,1)S(1)} %copy-done.1), custom_call_target="tpu_custom_call" | custom-call | tf_op jit(solution)/shard_map/route_blocks/pallas_call | solution.py:432
  8.0 0.0 copy-start.5
  8.0 107.2 %gathered_gram.1.gram = f32[4608,128]{1,0:T(8,128)} custom-call(bf16[2048,1024]{1,0:T(8,128)(2,1)} %bitcast.16), custom_call_target="tpu_custom_call" | custom-call | tf_op jit(solution)/shard_map/gathered_gram/pallas_call | solution.py:452
  115.2 0.0 copy-done.5
  115.2 0.0 copy-start.6
  115.3 0.0 copy-start.7
  115.3 0.0 copy-start
  115.3 1.7 copy-done
  116.9 15.0 %leaf_front.1 = (f32[128,1024]{1,0:T(8,128)}, f32[1280,128]{1,0:T(8,128)S(1)}) custom-call(s32[1]{0:T(128)} %bitcast.place, f32[4608,128]{1,0:T(8,128)S(1)} %copy-done, f32[1,1024]{1,0:T(1,128)S(1)} %slice_bitcast_fusion.weights), custom_call_target="tpu_custom_call" | custom-call | tf_op jit(solution)/shard_map/leaf_front/pallas_call | solution.py:498
  132.0 0.0 collective-permute-start
  132.0 0.5 collective-permute-start.1
  132.5 0.0 copy-done.6
  132.5 0.1 constant_dynamic-slice_fusion.3
  132.6 0.1 copy.14
  132.7 0.1 copy.13
  132.8 0.0 copy-done.7
  132.8 1.3 collective-permute-done.1
  134.1 0.1 collective-permute-start.2
  134.2 3.6 %collective-permute-done.2 = f32[1,1024]{1,0:T(1,128)S(1)} collective-permute-done((f32[1,1024]{1,0:T(1,128)S(1)}, f32[1,1024]{1,0:T(1,128)S(1)}, u32[]{:S(2)}, u32[]{:S(2)}) %collective-permute-start.2) | collective-permute-done | bytes 4128 | tf_op jit(solution)/shard_map/ppermute | solution.py:18
  137.8 0.0 collective-permute-done.other
  137.8 11.2 %mid_front.1 = (f32[64,1024]{1,0:T(8,128)}, f32[1280,128]{1,0:T(8,128)S(1)}) custom-call(s32[1]{0:T(128)} %bitcast.5.place, s32[2,4]{1,0:T(2,128)S(1)} %pad_add_fusion.maps, f32[1280,128]{1,0:T(8,128)S(1)} %get-tuple-element.8.own, f32[1280,128]{1,0:T(8,128)S(1)} %collective-permute-done.other, f32[1,1024]{1,0:T(1,128)S(1)} %get-tuple-element.12.weights), custom_call_target="tpu_custom_call" | custom-call | tf_op jit(solution)/shard_map/mid_front/pallas_call | solution.py:517
  149.0 14.3 %swap_leaves.1.other = f32[1280,128]{1,0:T(8,128)S(1)} custom-call(f32[1280,128]{1,0:T(8,128)S(1)} %get-tuple-element.10.own), custom_call_target="tpu_custom_call" | custom-call | tf_op jit(solution)/shard_map/swap_leaves/pallas_call | solution.py:479
  163.3 23.0 %top_front.1 = f32[64,1024]{1,0:T(8,128)} custom-call(s32[1]{0:T(128)} %bitcast.8.place, s32[2,4]{1,0:T(2,128)S(1)} %pad_add_fusion.1.maps, f32[1280,128]{1,0:T(8,128)S(1)} %get-tuple-element.10.own, f32[1280,128]{1,0:T(8,128)S(1)} %swap_leaves.1.other, f32[1,1024]{1,0:T(1,128)S(1)} %get-tuple-element.11.weights), custom_call_target="tpu_custom_call" | custom-call | tf_op jit(solution)/shard_map/top_front/pallas_call | solution.py:517
  (9 shorter events, 0.1 us)
Async XLA Ops:
  0.6 1.6 copy-start.1
  2.2 0.7 copy-start.2
  2.9 0.7 copy-start.3
  3.6 0.7 copy-start.4
  8.0 107.2 %copy-start.5 = (f32[1,3,1024]{2,0,1:T(1,128)S(1)}, f32[1,3,1024]{2,0,1:T(1,128)}, u32[]{:S(2)}) copy-start(f32[1,3,1024]{2,0,1:T(1,128)} %param.13) | copy-start | bytes 36868
  115.2 17.3 %copy-start.6 = (s32[8,4]{0,1:T(4,128)S(1)}, s32[8,4]{0,1:T(4,128)}, u32[]{:S(2)}) copy-start(s32[8,4]{0,1:T(4,128)} %param.11) | copy-start | bytes 388
  115.3 17.5 %copy-start.7 = (s32[4,4]{1,0:T(4,128)S(1)}, s32[4,4]{1,0:T(4,128)}, u32[]{:S(2)}) copy-start(s32[4,4]{1,0:T(4,128)} %param.12) | copy-start | bytes 196
  115.3 1.7 copy-start
  132.0 5.8 %collective-permute-start = (f32[1280,128]{1,0:T(8,128)S(1)}, f32[1280,128]{1,0:T(8,128)S(1)}, u32[]{:S(2)}, u32[]{:S(2)}) collective-permute-start(f32[1280,128]{1,0:T(8,128)S(1)} %get-tuple-element.8.own), channel_id=1, source_target_pairs={{0,4},{4,0},{8,12},{12,8},{16,20},{20,16},{24,28},{28,24},{1,5},{5... | collective-permute-start | bytes 1966088 | tf_op jit(solution)/shard_map/ppermute | solution.py:18
  132.0 2.1 %collective-permute-start.1 = (f32[2,1024]{1,0:T(2,128)S(1)}, f32[2,1024]{1,0:T(2,128)S(1)}, u32[]{:S(2)}, u32[]{:S(2)}) collective-permute-start(f32[2,1024]{1,0:T(2,128)S(1)} %bitcast.18), channel_id=1, source_target_pairs={{0,4},{4,0},{8,12},{12,8},{16,20},{20,16},{24,28},{28,24},{1,5},{5... | collective-permute-start | bytes 24584 | tf_op jit(solution)/shard_map/ppermute | solution.py:18
  134.1 3.7 %collective-permute-start.2 = (f32[1,1024]{1,0:T(1,128)S(1)}, f32[1,1024]{1,0:T(1,128)S(1)}, u32[]{:S(2)}, u32[]{:S(2)}) collective-permute-start(f32[1,1024]{1,0:T(1,128)S(1)} %slice.18), channel_id=1, source_target_pairs={{0,8},{4,12},{8,0},{12,4},{16,24},{20,28},{24,16},{28,20},{1,9},{5... | collective-permute-start | bytes 12296 | tf_op jit(solution)/shard_map/ppermute | solution.py:18

commit v4 on v3

--- a/solution.py
+++ b/solution.py
@@ -181,14 +181,14 @@
     ]
 
 
-def add_weights(front, weights, block):
+def add_weights(front, weight_of, block):
     size = front.shape[0]
     same = lax.broadcasted_iota(jnp.int32, (block, block), 0) == lax.broadcasted_iota(
         jnp.int32, (block, block), 1
     )
     for start in range(0, size, block):
         at = slice(start, start + block)
-        front[at, at] = front[at, at] + jnp.where(same, weights[:, at], 0.0)
+        front[at, at] = front[at, at] + jnp.where(same, weight_of(start // block), 0.0)
 
 
 def take_rows(front, out, start):
@@ -211,43 +211,77 @@
         ]
 
 
-def leaf_kernel(block, place, gram, weights, out, rest, front, diagonal, over, under):
+def carry_rows(packed, base, rows):
+    packed[base:, :] = jnp.zeros((packed.shape[0] - base, packed.shape[1]), packed.dtype)
+    for index, row in enumerate(rows):
+        packed[base + index : base + index + 1, :] = row
+
+
+def leaf_kernel(block, gram, weights, out, rest, front, diagonal, over, under):
     width = front.shape[0]
-    front[...] = jnp.zeros_like(front)
-    for index, (i, j) in enumerate(pairs(width // block)):
+    blocks = width // block
+    for index, (i, j) in enumerate(pairs(blocks)):
         front[i * block : (i + 1) * block, j * block : (j + 1) * block] = gram[
             index * block : (index + 1) * block, :
         ]
-    add_weights(front, weights, block)
+
+    def weight_of(level, b):
+        return weights[level : level + 1, b * block : (b + 1) * block]
+
+    add_weights(front, functools.partial(weight_of, 0), block)
+    base = len(pairs(blocks // 2)) * block
+    carry_rows(rest, base, [weight_of(level, b) for level in (1, 2) for b in range(blocks)])
     eliminate(front, diagonal, over, under, width // 2, block)
-    take_rows(front, out, pl.multiple_of(place[0] * out.shape[0], SUB))
-    pack_triangle(front, rest, width // 2 // block, block)
-
-
-def merge_kernel(block, pivots, place, maps, own, other, weights, out, *more):
+    take_rows(front, out, pl.multiple_of(lax.axis_index("front") * out.shape[0], SUB))
+    pack_triangle(front, rest, blocks // 2, block)
+
+
+def merge_kernel(block, pivots, fronts, level, maps, own, other, out, *more):
     *more, front, diagonal, over, under = more
-    half = front.shape[0] // 2
+    width = front.shape[0]
+    half = width // 2
+    blocks = width // block
+    base = len(pairs(blocks // 2)) * block
+    leaf = lax.axis_index("leaf")
+    below = 2 ** (level - 1)
+    mine = leaf // below
+    theirs = mine + 1 - 2 * lax.rem(mine, 2)
     front[...] = jnp.zeros_like(front)
-    add_weights(front, weights, block)
-    for source, child in enumerate((own, other)):
+    add_weights(front, lambda b: own[base + b : base + b + 1, :] + other[base + b : base + b + 1, :], block)
+    for source, child in ((mine, own), (theirs, other)):
         for index, (i, j) in enumerate(pairs(half // block)):
             tile = child[index * block : (index + 1) * block, :]
-            first = pl.ds(pl.multiple_of(maps[source, i] * block, block), block)
-            second = pl.ds(pl.multiple_of(maps[source, j] * block, block), block)
-            front[first, second] = front[first, second] + tile
-            if i != j:
+            row, column = maps[source, i], maps[source, j]
+            first = pl.ds(pl.multiple_of(row * block, block), block)
+            second = pl.ds(pl.multiple_of(column * block, block), block)
+
+            def plain(first=first, second=second, tile=tile):
+                front[first, second] = front[first, second] + tile
+
+            def turned(first=first, second=second, tile=tile):
                 front[second, first] = front[second, first] + tile.T
 
+            if i == j:
+                plain()
+            else:
+                pl.when(row < column)(plain)
+                pl.when(row > column)(turned)
+
     def touched(index):
-        found = maps[0, 0] == index
-        for source in range(2):
+        found = maps[mine, 0] == index
+        for source in (mine, theirs):
             for i in range(half // block):
                 found = jnp.logical_or(found, maps[source, i] == index)
         return found
 
     eliminate(front, diagonal, over, under, pivots, block, touched)
-    take_rows(front, out, pl.multiple_of(place[0] * out.shape[0], SUB))
+    turn = lax.rem(leaf, 2**level) * fronts + lax.axis_index("front")
+    take_rows(front, out, pl.multiple_of(turn * out.shape[0], SUB))
     if more:
+        carry_rows(more[0], base, [
+            own[base + b : base + b + 1, :] + other[base + b : base + b + 1, :]
+            for b in range(blocks, 2 * blocks)
+        ])
         pack_triangle(front, more[0], half // block, block)
 
 
@@ -287,7 +321,8 @@
 
 
 def sum_kernel(
-    leaves, fronts, block, rows, out, far_rows, own_rows, far, own, landed, swapped, full,
+    leaves, fronts, block, order, assign, pattern, blocks, out,
+    rows, far_rows, own_rows, far, own, landed, swapped, full,
     far_send, far_recv, own_send, own_recv, kept, send, recv, swap_send, swap_recv, send_back, recv_back,
 ):
     leaf, me = lax.axis_index("leaf"), lax.axis_index("front")
@@ -310,10 +345,13 @@
 
     def gather(base, target, send, recv, slot):
         place = target.at[at(mate * depth, depth)]
-        copies = [
-            remote(rows.at[at((base + other) * depth, depth)], place, send.at[d], recv.at[d], (here + other, me))
-            for d, other in enumerate(mates)
-        ]
+        copies = []
+        for d, other in enumerate(mates):
+            route_slot(order, assign, pattern, blocks, rows, base + other)
+            copies.append(remote(
+                rows.at[at((base + other) * depth, depth)], place, send.at[d], recv.at[d], (here + other, me)
+            ))
+        route_slot(order, assign, pattern, blocks, rows, base + mate)
         stay = pltpu.make_async_copy(rows.at[at((base + mate) * depth, depth)], place, kept.at[slot])
         stay.start()
         return copies + [stay]
@@ -381,30 +419,25 @@
     out[...] = full[...]
 
 
-def route_kernel(order, assign, pattern, blocks, out):
-    leaves, positions = out.shape[:2]
-    count, _, width = blocks.shape
+def route_slot(order, assign, pattern, blocks, rows, slot):
+    count, size, width = blocks.shape
     column_blocks = pattern.shape[1]
     block = width // column_blocks
-
-    def slot_step(slot, carry):
-        found = [jnp.int32(count)] * positions
-        for b in range(count):
-            free = assign[b] == order[slot]
-            for p in range(positions):
-                take = jnp.logical_and(free, found[p] == count)
-                found[p] = jnp.where(take, b, found[p])
-                free = jnp.logical_and(free, jnp.logical_not(take))
-        for p in range(positions):
-            source = jnp.minimum(found[p], count - 1)
-            for c in range(column_blocks):
-                keep = jnp.where(found[p] < count, pattern[source, c], 0)
-                cols = slice(c * block, (c + 1) * block)
-                scale = jnp.full((block, block), keep, jnp.int32).astype(jnp.float32)
-                out[slot, p, :, cols] = blocks[source, :, cols] * scale.astype(out.dtype)
-        return carry
-
-    lax.fori_loop(0, leaves, slot_step, 0)
+    found = [jnp.int32(count)] * CAP
+    for b in range(count):
+        free = assign[b] == order[slot]
+        for p in range(CAP):
+            take = jnp.logical_and(free, found[p] == count)
+            found[p] = jnp.where(take, b, found[p])
+            free = jnp.logical_and(free, jnp.logical_not(take))
+    for p in range(CAP):
+        source = jnp.minimum(found[p], count - 1)
+        place = pl.ds(pl.multiple_of((slot * CAP + p) * size, size), size)
+        for c in range(column_blocks):
+            keep = jnp.where(found[p] < count, pattern[source, c], 0)
+            cols = slice(c * block, (c + 1) * block)
+            scale = jnp.full((size, block), keep, jnp.int32).astype(jnp.float32)
+            rows[place, cols] = blocks[source, :, cols] * scale.astype(rows.dtype)
 
 
 def swap_kernel(fronts, stride, own, out, got, send, recv, send_on, recv_on):
@@ -428,23 +461,13 @@
 VMEM = pl.BlockSpec(memory_space=pltpu.VMEM)
 
 
-def route(order, assign, pattern, blocks, leaves):
-    return pl.pallas_call(
-        route_kernel,
-        out_shape=jax.ShapeDtypeStruct((leaves, CAP) + blocks.shape[1:], blocks.dtype),
-        in_specs=[SMEM, SMEM, SMEM, VMEM],
-        out_specs=VMEM,
-        compiler_params=pltpu.CompilerParams(vmem_limit_bytes=48 * 2**20),
-        name="route_blocks",
-    )(order, assign.reshape(-1), pattern, blocks)
-
-
-def gathered_gram(rows, leaves, fronts, block):
-    width = rows.shape[1]
+def gathered_gram(order, assign, pattern, blocks, leaves, fronts):
+    _, block, width = blocks.shape
     packed = (len(pairs(width // block)) * block, block)
     team = leaves // 2
     levels = fronts.bit_length() - 1
-    half_rows = (rows.shape[0] // 2, width)
+    depth = CAP * block
+    half_rows = (team * depth, width)
 
     def many(count):
         return pltpu.SemaphoreType.DMA((count,))
@@ -452,11 +475,12 @@
     return pl.pallas_call(
         functools.partial(sum_kernel, leaves, fronts, block),
         out_shape=jax.ShapeDtypeStruct(packed, jnp.float32),
-        in_specs=[VMEM],
+        in_specs=[SMEM, SMEM, SMEM, VMEM],
         out_specs=VMEM,
         scratch_shapes=[
-            pltpu.VMEM(half_rows, rows.dtype),
-            pltpu.VMEM(half_rows, rows.dtype),
+            pltpu.VMEM((leaves * depth, width), blocks.dtype),
+            pltpu.VMEM(half_rows, blocks.dtype),
+            pltpu.VMEM(half_rows, blocks.dtype),
             pltpu.VMEM(packed, jnp.float32),
             pltpu.VMEM(packed, jnp.float32),
             pltpu.VMEM((2,) + packed, jnp.float32),
@@ -470,7 +494,7 @@
             collective_id=0, has_side_effects=True, vmem_limit_bytes=56 * 2**20
         ),
         name="gathered_gram",
-    )(rows)
+    )(order, assign.reshape(-1), pattern, blocks)
 
 
 def swap_leaves(own, fronts, stride):
@@ -489,82 +513,55 @@
     )(own)
 
 
-def triangle_shape(width, block):
-    return jax.ShapeDtypeStruct((len(pairs(width // 2 // block)) * block, block), jnp.float32)
-
-
-def leaf_level(gram, weights, place, rows, block):
+def triangle_shape(width, block, fronts):
+    rows = len(pairs(width // 2 // block)) * block + max(2 * (width // block), SUB * fronts)
+    return jax.ShapeDtypeStruct((rows, block), jnp.float32)
+
+
+def leaf_level(gram, weights, rows, block, fronts):
     width = weights.shape[1]
     return pl.pallas_call(
         functools.partial(leaf_kernel, block),
         out_shape=(
             jax.ShapeDtypeStruct((rows, width), jnp.float32),
-            triangle_shape(width, block),
+            triangle_shape(width, block, fronts),
         ),
-        in_specs=[SMEM, VMEM, VMEM],
+        in_specs=[VMEM, VMEM],
         out_specs=(VMEM, VMEM),
         scratch_shapes=work(width, block),
         compiler_params=pltpu.CompilerParams(vmem_limit_bytes=48 * 2**20),
         name="leaf_front",
-    )(place.reshape(1).astype(jnp.int32), gram, weights)
-
-
-def merge_level(own, other, maps, weights, place, rows, block, pivots, name):
-    width = weights.shape[1]
+    )(gram, weights)
+
+
+def merge_level(own, other, maps, rows, width, block, pivots, fronts, level, name):
     outs = [jax.ShapeDtypeStruct((rows, width), jnp.float32)]
     if pivots < width:
-        outs.append(triangle_shape(width, block))
+        outs.append(triangle_shape(width, block, fronts))
     return pl.pallas_call(
-        functools.partial(merge_kernel, block, pivots),
+        functools.partial(merge_kernel, block, pivots, fronts, level),
         out_shape=tuple(outs),
-        in_specs=[SMEM, SMEM, VMEM, VMEM, VMEM],
+        in_specs=[SMEM, VMEM, VMEM],
         out_specs=tuple([VMEM] * len(outs)),
         scratch_shapes=work(width, block),
         compiler_params=pltpu.CompilerParams(vmem_limit_bytes=48 * 2**20),
         name=name,
-    )(place.reshape(1).astype(jnp.int32), maps, own, other, weights)
+    )(maps, own, other)
 
 
 def local(blocks, pattern, assign, order, leaf_map, mid_map, prior):
     leaves = lax.axis_size("leaf")
     fronts = lax.axis_size("front")
-    slot_index = lax.axis_index("leaf")
-    front_index = lax.axis_index("front")
-    local_blocks, block_size, full_width = blocks.shape
+    block_size, full_width = blocks.shape[1:]
     half_width = full_width // 2
-    quarter = full_width // 4
-    carried = prior[0, 1:3]
-    carried = carried + partner(carried, "leaf", 0)
-    top_weights = carried[1:2] + partner(carried[1:2], "leaf", 1)
-    outgoing = route(order, assign, pattern, blocks, leaves)
-    gram = gathered_gram(outgoing.reshape(-1, full_width), leaves, fronts, block_size)
-    leaf_out, rest = leaf_level(
-        gram, prior[0, 0:1], front_index, half_width // fronts, block_size
-    )
-    piece_rows = quarter // fronts
-    partner_slot = jnp.bitwise_xor(slot_index, 1)
+    piece_rows = full_width // 4 // fronts
+    gram = gathered_gram(order, assign, pattern, blocks, leaves, fronts)
+    leaf_out, rest = leaf_level(gram, prior[0], half_width // fronts, block_size, fronts)
     mid_out, mid_rest = merge_level(
-        rest,
-        partner(rest, "leaf", 0),
-        jnp.stack([leaf_map[slot_index], leaf_map[partner_slot]]),
-        carried[0:1],
-        slot_index % 2 * fronts + front_index,
-        piece_rows,
-        block_size,
-        half_width,
-        "mid_front",
-    )
-    middle = slot_index // 2
-    other_middle = jnp.bitwise_xor(slot_index, 2) // 2
+        rest, partner(rest, "leaf", 0), leaf_map, piece_rows, full_width, block_size, half_width, fronts, 1, "mid_front"
+    )
     (top_out,) = merge_level(
-        mid_rest,
-        swap_leaves(mid_rest, fronts, 2),
-        jnp.stack([mid_map[middle], mid_map[other_middle]]),
-        top_weights,
-        slot_index % 4 * fronts + front_index,
-        piece_rows,
-        block_size,
-        full_width,
+        mid_rest, swap_leaves(mid_rest, fronts, 2), mid_map, piece_rows, full_width, block_size, full_width, fronts, 2,
         "top_front",
     )
     return (leaf_out[None], mid_out[None], top_out[None])

time: 187 us -> 179 us (0.957)
  local copies, waits for them, and re-layouts: 5.54 us -> 2.46 us
  Pallas kernels: 175 us -> 172 us
  waiting for transfers between devices: 4.83 us -> 2.03 us
    unnamed x19 -> x8, local copies, waits for them, and re-layouts: 5.45 us -> 2.46 us
    ppermute x3 -> x1, waiting for transfers between devices: 4.83 us -> 2.03 us  [partner(): return lax.ppermute(value, axis, pairs)]
    pallas_call x3 -> x2, Pallas kernels: 38 us -> 35.5 us  [merge_level(): pl.pallas_call(functools.partial(merge_kernel, block, pivots, fronts, lev...]
  transfers between devices with their start and end apart: 3 -> 1, of which waited for: 2 -> 1; matrix products, arithmetic and copies ran while one was open for 0% -> 0% of each run, Pallas kernels for 0% -> 0%
where the time goes in v4:
time: 179 us; the launch traced here: 178 us
  Pallas kernels  172 us (96%)
  local copies, waits for them, and re-layouts  2.46 us (1%)
  waiting for transfers between devices  2.03 us (1%)
    pallas_call x1, Pallas kernels, gathered_gram(): pl.pallas_call(functools.partial(sum_kernel, leaves, fronts, block), out_...  107 us
    pallas_call x2, Pallas kernels, merge_level(): pl.pallas_call(functools.partial(merge_kernel, block, pivots, fronts, lev...  35.5 us
    pallas_call x1, Pallas kernels, swap_leaves(): pl.pallas_call(functools.partial(swap_kernel, fronts, stride), out_shape=...  15 us
    pallas_call x1, Pallas kernels, leaf_level(): pl.pallas_call(functools.partial(leaf_kernel, block), out_shape=(jax.Shap...  14.9 us
  transfers between devices with their start and end apart: 1, of which 1 were waited for; matrix products, arithmetic and copies ran while one was open for 0% of the time, Pallas kernels for 0%

profile of v4, /device:TPU:0, one launch (start us, length us, event | category | flops | bytes accessed | tf_op | source)
XLA Modules:
  0.0 177.6 jit_solution(6571218643418743478)
XLA Ops:
  0.6 0.7 copy.13
  1.3 0.0 copy-start.2
  1.3 107.0 %gathered_gram.1.gram = f32[4608,128]{1,0:T(8,128)} custom-call(s32[8]{0:T(128)} %order.1, s32[8]{0:T(128)} %bitcast.9, s32[8,8]{1,0:T(8,128)} %pattern.1, bf16[8,128,1024]{2,1,0:T(8,128)(2,1)} %blocks.1), custom_call_target="tpu_custom_call" | custom-call | tf_op jit(solution)/shard_map/gathered_gram/pallas_call | solution.py:475
  108.4 0.0 copy-start
  108.4 1.7 copy-done
  110.0 0.0 copy-start.1
  110.0 14.9 %leaf_front.1 = (f32[128,1024]{1,0:T(8,128)}, f32[1312,128]{1,0:T(8,128)S(1)}) custom-call(f32[4608,128]{1,0:T(8,128)S(1)} %copy-done, f32[3,1024]{1,0:T(4,128)S(1)} %bitcast.7), custom_call_target="tpu_custom_call" | custom-call | tf_op jit(solution)/shard_map/leaf_front/pallas_call | solution.py:523
  124.9 0.0 collective-permute-start
  124.9 0.0 copy-done.2
  124.9 0.1 copy.10.maps
  125.0 2.0 %collective-permute-done.other = f32[1312,128]{1,0:T(8,128)S(1)} collective-permute-done((f32[1312,128]{1,0:T(8,128)S(1)}, f32[1312,128]{1,0:T(8,128)S(1)}, u32[]{:S(2)}, u32[]{:S(2)}) %collective-permute-start) | collective-permute-done | bytes 671776 | tf_op jit(solution)/shard_map/ppermute | solution.py:18
  127.0 11.7 %mid_front.1 = (f32[64,1024]{1,0:T(8,128)}, f32[1312,128]{1,0:T(8,128)S(1)}) custom-call(s32[8,4]{1,0:T(8,128)S(1)} %copy.10.maps, f32[1312,128]{1,0:T(8,128)S(1)} %get-tuple-element.8.own, f32[1312,128]{1,0:T(8,128)S(1)} %collective-permute-done.other), custom_call_target="tpu_custom_call" | custom-call | tf_op jit(solution)/shard_map/mid_front/pallas_call | solution.py:541
  138.7 15.0 %swap_leaves.1.other = f32[1312,128]{1,0:T(8,128)S(1)} custom-call(f32[1312,128]{1,0:T(8,128)S(1)} %get-tuple-element.10.own), custom_call_target="tpu_custom_call" | custom-call | tf_op jit(solution)/shard_map/swap_leaves/pallas_call | solution.py:503
  153.8 0.0 copy-done.1
  153.8 23.8 %top_front.1 = f32[64,1024]{1,0:T(8,128)} custom-call(s32[4,4]{1,0:T(4,128)S(1)} %copy-done.1, f32[1312,128]{1,0:T(8,128)S(1)} %get-tuple-element.10.own, f32[1312,128]{1,0:T(8,128)S(1)} %swap_leaves.1.other), custom_call_target="tpu_custom_call" | custom-call | tf_op jit(solution)/shard_map/top_front/pallas_call | solution.py:541
Async XLA Ops:
  1.3 123.6 %copy-start.2 = (s32[8,4]{0,1:T(4,128)S(1)}, s32[8,4]{0,1:T(4,128)}, u32[]{:S(2)}) copy-start(s32[8,4]{0,1:T(4,128)} %param.11) | copy-start | bytes 388
  108.4 1.7 copy-start
  110.0 43.7 %copy-start.1 = (s32[4,4]{1,0:T(4,128)S(1)}, s32[4,4]{1,0:T(4,128)}, u32[]{:S(2)}) copy-start(s32[4,4]{1,0:T(4,128)} %maps.2) | copy-start | bytes 196
  124.9 2.1 %collective-permute-start = (f32[1312,128]{1,0:T(8,128)S(1)}, f32[1312,128]{1,0:T(8,128)S(1)}, u32[]{:S(2)}, u32[]{:S(2)}) collective-permute-start(f32[1312,128]{1,0:T(8,128)S(1)} %get-tuple-element.8.own), channel_id=1, source_target_pairs={{0,4},{4,0},{8,12},{12,8},{16,20},{20,16},{24,28},{28,24},{1,5},{5... | collective-permute-start | bytes 2015240 | tf_op jit(solution)/shard_map/ppermute | solution.py:18

commit v5 on v4

--- a/solution.py
+++ b/solution.py
@@ -491,7 +491,7 @@
             many(2 * levels), many(2 * levels),
         ],
         compiler_params=pltpu.CompilerParams(
-            collective_id=0, has_side_effects=True, vmem_limit_bytes=56 * 2**20
+            collective_id=0, has_side_effects=True, vmem_limit_bytes=40 * 2**20
         ),
         name="gathered_gram",
     )(order, assign.reshape(-1), pattern, blocks)

time: 179 us -> 180 us (level); the launches traced: 178 us -> 181 us
  Pallas kernels: 172 us -> 174 us
  local copies, waits for them, and re-layouts: 2.46 us -> 4.39 us
    pallas_call x2, Pallas kernels: 35.5 us -> 40.9 us  [merge_level(): pl.pallas_call(functools.partial(merge_kernel, block, pivots, fronts, lev...]
    pallas_call x1, Pallas kernels: 107 us -> 105 us  [gathered_gram(): pl.pallas_call(functools.partial(sum_kernel, leaves, fronts, block), out_...]
    unnamed x8 -> x14, local copies, waits for them, and re-layouts: 2.46 us -> 4.39 us
where the time goes in v5:
time: 180 us; the launch traced here: 181 us
  Pallas kernels  174 us (97%)
  local copies, waits for them, and re-layouts  4.39 us (2%)
  waiting for transfers between devices  2.03 us (1%)
    pallas_call x1, Pallas kernels, gathered_gram(): pl.pallas_call(functools.partial(sum_kernel, leaves, fronts, block), out_...  105 us
    pallas_call x2, Pallas kernels, merge_level(): pl.pallas_call(functools.partial(merge_kernel, block, pivots, fronts, lev...  40.9 us
    pallas_call x1, Pallas kernels, leaf_level(): pl.pallas_call(functools.partial(leaf_kernel, block), out_shape=(jax.Shap...  14.9 us
    pallas_call x1, Pallas kernels, swap_leaves(): pl.pallas_call(functools.partial(swap_kernel, fronts, stride), out_shape=...  13.5 us
    unnamed x14, local copies, waits for them, and re-layouts  4.39 us
  transfers between devices with their start and end apart: 1, of which 1 were waited for; matrix products, arithmetic and copies ran while one was open for 0% of the time, Pallas kernels for 0%

profile of v5, /device:TPU:0, one launch (start us, length us, event | category | flops | bytes accessed | tf_op | source)
XLA Modules:
  0.0 180.9 jit_solution(11759705206573005734)
XLA Ops:
  0.6 0.7 copy.13
  1.3 0.0 copy-start
  1.3 1.6 copy-done
  2.9 0.0 copy-start.1
  2.9 0.7 copy-done.1
  3.6 0.0 copy-start.3
  3.6 0.7 copy-done.3
  4.3 0.0 copy-start.4
  4.3 0.7 copy-done.4
  4.9 0.0 copy-start.5
  4.9 104.6 %gathered_gram.1.gram = f32[4608,128]{1,0:T(8,128)S(1)} custom-call(s32[8]{0:T(128)S(1)} %copy-done.3, s32[8]{0:T(128)S(1)} %bitcast.8, s32[8,8]{1,0:T(8,128)S(1)} %copy-done.1, bf16[8,128,1024]{2,1,0:T(8,128)(2,1)S(1)} %copy-done), custom_call_target="tpu_custom_call" | custom-call | tf_op jit(solution)/shard_map/gathered_gram/pallas_call | solution.py:475
  109.5 0.0 copy-start.2
  109.5 14.9 %leaf_front.1 = (f32[128,1024]{1,0:T(8,128)}, f32[1312,128]{1,0:T(8,128)S(1)}) custom-call(f32[4608,128]{1,0:T(8,128)S(1)} %gathered_gram.1.gram, f32[3,1024]{1,0:T(4,128)S(1)} %bitcast.7), custom_call_target="tpu_custom_call" | custom-call | tf_op jit(solution)/shard_map/leaf_front/pallas_call | solution.py:523
  124.4 0.0 collective-permute-start
  124.4 0.0 copy-done.5
  124.4 0.1 copy.10.maps
  124.5 2.0 %collective-permute-done.other = f32[1312,128]{1,0:T(8,128)S(1)} collective-permute-done((f32[1312,128]{1,0:T(8,128)S(1)}, f32[1312,128]{1,0:T(8,128)S(1)}, u32[]{:S(2)}, u32[]{:S(2)}) %collective-permute-start) | collective-permute-done | bytes 671776 | tf_op jit(solution)/shard_map/ppermute | solution.py:18
  126.5 16.5 %mid_front.1 = (f32[64,1024]{1,0:T(8,128)}, f32[1312,128]{1,0:T(8,128)S(1)}) custom-call(s32[8,4]{1,0:T(8,128)S(1)} %copy.10.maps, f32[1312,128]{1,0:T(8,128)S(1)} %get-tuple-element.8.own, f32[1312,128]{1,0:T(8,128)S(1)} %collective-permute-done.other), custom_call_target="tpu_custom_call" | custom-call | tf_op jit(solution)/shard_map/mid_front/pallas_call | solution.py:541
  143.1 13.5 %swap_leaves.1.other = f32[1312,128]{1,0:T(8,128)S(1)} custom-call(f32[1312,128]{1,0:T(8,128)S(1)} %get-tuple-element.10.own), custom_call_target="tpu_custom_call" | custom-call | tf_op jit(solution)/shard_map/swap_leaves/pallas_call | solution.py:503
  156.5 0.0 copy-done.2
  156.5 24.4 %top_front.1 = f32[64,1024]{1,0:T(8,128)} custom-call(s32[4,4]{1,0:T(4,128)S(1)} %copy-done.2, f32[1312,128]{1,0:T(8,128)S(1)} %get-tuple-element.10.own, f32[1312,128]{1,0:T(8,128)S(1)} %swap_leaves.1.other), custom_call_target="tpu_custom_call" | custom-call | tf_op jit(solution)/shard_map/top_front/pallas_call | solution.py:541
Async XLA Ops:
  1.3 1.6 copy-start
  2.9 0.7 copy-start.1
  3.6 0.7 copy-start.3
  4.3 0.7 copy-start.4
  4.9 119.5 %copy-start.5 = (s32[8,4]{0,1:T(4,128)S(1)}, s32[8,4]{0,1:T(4,128)}, u32[]{:S(2)}) copy-start(s32[8,4]{0,1:T(4,128)} %param.11) | copy-start | bytes 388
  109.5 47.0 %copy-start.2 = (s32[4,4]{1,0:T(4,128)S(1)}, s32[4,4]{1,0:T(4,128)}, u32[]{:S(2)}) copy-start(s32[4,4]{1,0:T(4,128)} %maps.2) | copy-start | bytes 196
  124.4 2.1 %collective-permute-start = (f32[1312,128]{1,0:T(8,128)S(1)}, f32[1312,128]{1,0:T(8,128)S(1)}, u32[]{:S(2)}, u32[]{:S(2)}) collective-permute-start(f32[1312,128]{1,0:T(8,128)S(1)} %get-tuple-element.8.own), channel_id=1, source_target_pairs={{0,4},{4,0},{8,12},{12,8},{16,20},{20,16},{24,28},{28,24},{1,5},{5... | collective-permute-start | bytes 2015240 | tf_op jit(solution)/shard_map/ppermute | solution.py:18
